TPU v7x, 256 devices: a whole 4x4x8 slice. The times are simulated.
256 devices in a mesh: chain: 32 (over z_lo, x, core), dp: 8 (over z_hi, y).
Axes of the slice: x: 4, y: 4, z: 8 (z_hi: 2, z_lo: 4; z = z_hi * 4 + z_lo), core: 2. Of those that a mesh axis runs over, the one named last changes fastest.
Arguments:
- segments: bfloat16 [8, 32, 128, 1024], P('dp', 'chain'), may hold values from -6 to 6
- lengths: int32 [8, 32], P('dp', 'chain'), may hold values from 64 to 128, as said below
- query_weight: bfloat16 [1024, 1024], replicated, may hold values from -0.1875 to 0.1875
- key_weight: bfloat16 [1024, 256], replicated, may hold values from -0.1875 to 0.1875
- value_weight: bfloat16 [1024, 256], replicated, may hold values from -0.1875 to 0.1875
- out_weight: bfloat16 [1024, 1024], replicated, may hold values from -0.1875 to 0.1875
- norm_gain: float32 [1024], replicated, may hold values from 0.5 to 1.5
- gate_vector: float32 [1024], replicated, may hold values from -0.6 to 0.6
- gate_bias: float32 [128], replicated, may hold values from -2 to 5
- memory_init: bfloat16 [128, 1024], replicated, may hold values from -6 to 6
- cotangent: bfloat16 [8, 32, 128, 1024], P('dp', 'chain'), may hold values from -6 to 6
Outputs:
- layer_output: bfloat16 [8, 32, 128, 1024], P('dp', 'chain')
- grad_query: float32 [1024, 1024], P(('chain', 'dp'))
- grad_key: float32 [1024, 256], P(('chain', 'dp'))
- grad_value: float32 [1024, 256], P(('chain', 'dp'))
- grad_out: float32 [1024, 1024], P(('chain', 'dp'))
- grad_gain: float32 [1024], P(('chain', 'dp'))
- grad_gate: float32 [1024], P(('chain', 'dp'))
- grad_memory: float32 [128, 1024], P(None, ('chain', 'dp'))
Inputs may be any that keep to these rules, and one draw needn't show every extreme that they name: `lengths`: in every document one segment is full.
All inputs are finite; a program needn't handle non-finite values.
Results may differ from a plain program's by a relative error of at most 0.02.
Values sent between devices are 32-bit elements; how exact they have to be, the bound alone decides.
A program may use at most 128 MiB of HBM per device.

v0:
```python
import jax
import jax.numpy as jnp
from jax import lax
from jax.sharding import Mesh
from jax.sharding import PartitionSpec as P

HEAD = 64
CHAIN = ("chain_0", "chain_1", "chain_2")
CHAIN_DP = ("chain_0", "chain_1", "chain_2", "dp")


epsilon = 1e-05
score_scale = 0.125


def filled_with(shard, identity):
    return jax.tree.map(
        lambda a, e: jnp.broadcast_to(jnp.asarray(e, a.dtype), a.shape), shard, identity
    )


def entering(shard, axes, combine, identity, reverse):
    before = start = filled_with(shard, identity)
    subtotal = shard
    for axis in reversed(axes):
        peers, place = (lax.axis_size(axis), lax.axis_index(axis))
        pieces = jax.tree.map(lambda part: lax.all_gather(part, axis), subtotal)
        inside, subtotal = (start, start)
        for k in reversed(range(peers)) if reverse else range(peers):
            passed = k > place if reverse else k < place
            subtotal = combine(subtotal, jax.tree.map(lambda part: part[k], pieces))
            inside = jax.tree.map(lambda new, old: jnp.where(passed, new, old), subtotal, inside)
        before = combine(inside, before)
    return before


def normalize(activations, norm_gain):
    inverse = lax.rsqrt(jnp.mean(activations * activations, axis=-1, keepdims=True) + epsilon)
    return (activations * inverse * norm_gain).astype(jnp.bfloat16)


def prepare(query_weight, key_weight, value_weight, norm_gain, segment):
    normed_rows = normalize(segment.astype(jnp.float32), norm_gain)
    queries = (
        jnp.dot(normed_rows, query_weight, preferred_element_type=jnp.float32) * score_scale
    ).astype(jnp.bfloat16)
    key_rows = jnp.dot(normed_rows, key_weight, preferred_element_type=jnp.float32).astype(
        jnp.bfloat16
    )
    value_rows = jnp.dot(normed_rows, value_weight, preferred_element_type=jnp.float32).astype(
        jnp.bfloat16
    )
    return (queries, key_rows, value_rows)


def attend(queries, key_rows, value_rows, allowed):
    count = queries.shape[0]
    width = key_rows.shape[0]
    groups = key_rows.shape[1] // HEAD
    shared = queries.shape[1] // key_rows.shape[1]
    grouped = queries.reshape(count, groups, shared, HEAD)
    keyed = key_rows.reshape(width, groups, HEAD)
    valued = value_rows.reshape(width, groups, HEAD)
    scores = jnp.einsum("rgsh,kgh->gsrk", grouped, keyed, preferred_element_type=jnp.float32)
    scores = jnp.where(allowed, scores, -1e30)
    weights = jax.nn.softmax(scores, axis=-1).astype(jnp.bfloat16)
    context = jnp.einsum("gsrk,kgh->rgsh", weights, valued, preferred_element_type=jnp.float32)
    return context.reshape(count, groups * shared * HEAD).astype(jnp.bfloat16)


def read_part(
    queries,
    seg_keys,
    seg_values,
    key_weight,
    value_weight,
    out_weight,
    norm_gain,
    memory_in,
    segment,
    seg_length,
):
    memory_rows = normalize(memory_in, norm_gain)
    memory_keys = jnp.dot(memory_rows, key_weight, preferred_element_type=jnp.float32).astype(
        jnp.bfloat16
    )
    memory_values = jnp.dot(memory_rows, value_weight, preferred_element_type=jnp.float32).astype(
        jnp.bfloat16
    )
    key_rows = jnp.concatenate([memory_keys, seg_keys], axis=0)
    value_rows = jnp.concatenate([memory_values, seg_values], axis=0)
    count = segment.shape[0]
    places = jnp.arange(count)
    causal = (places[None, :] <= places[:, None]) & (places[None, :] < seg_length)
    allowed = jnp.concatenate([jnp.ones((count, memory_in.shape[0]), dtype=bool), causal], axis=1)
    context = attend(queries, key_rows, value_rows, allowed)
    return segment.astype(jnp.float32) + jnp.dot(
        context, out_weight, preferred_element_type=jnp.float32
    )


def write_part(
    seg_keys,
    seg_values,
    query_weight,
    out_weight,
    norm_gain,
    gate_vector,
    memory_start,
    gate_bias,
    seg_length,
):
    start_rows = normalize(memory_start, norm_gain)
    slot_queries = (
        jnp.dot(start_rows, query_weight, preferred_element_type=jnp.float32) * score_scale
    ).astype(jnp.bfloat16)
    places = jnp.arange(seg_keys.shape[0])
    allowed = jnp.broadcast_to(
        places[None, :] < seg_length, (memory_start.shape[0], seg_keys.shape[0])
    )
    context = attend(slot_queries, seg_keys, seg_values, allowed)
    written = jnp.dot(context, out_weight, preferred_element_type=jnp.float32)
    retain = jax.nn.sigmoid(
        gate_bias + jnp.dot(written, gate_vector, precision=lax.Precision.HIGHEST)
    )
    return (retain, written)


def compose(earlier, later):
    keep_early, add_early = earlier
    keep_later, add_later = later
    return (keep_early * keep_later, keep_later[:, None] * add_early + add_later)


def per_device(
    segments,
    lengths,
    query_weight,
    key_weight,
    value_weight,
    out_weight,
    norm_gain,
    gate_vector,
    gate_bias,
    memory_init,
    cotangent,
):
    segment = segments[0, 0]
    seg_length = lengths[0, 0]
    memory_start = memory_init.astype(jnp.float32)

    def prepared(query_part, key_part, value_part, gain_part):
        return prepare(query_part, key_part, value_part, gain_part, segment)

    (queries, seg_keys, seg_values), prep_back = jax.vjp(
        prepared, query_weight, key_weight, value_weight, norm_gain
    )

    def writing(keys_in, values_in, query_part, out_part, gain_part, vector_part, start_part):
        return write_part(
            keys_in,
            values_in,
            query_part,
            out_part,
            gain_part,
            vector_part,
            start_part,
            gate_bias,
            seg_length,
        )

    (retain, written), write_back = jax.vjp(
        writing,
        seg_keys,
        seg_values,
        query_weight,
        out_weight,
        norm_gain,
        gate_vector,
        memory_start,
    )
    identity = (jnp.ones_like(retain), jnp.zeros_like(written))
    prefix_keep, prefix_add = entering(
        (retain, (1.0 - retain)[:, None] * written), CHAIN, compose, identity, False
    )
    memory_in = prefix_keep[:, None] * memory_start + prefix_add

    def reading(
        queries_in, keys_in, values_in, key_part, value_part, out_part, gain_part, memory_part
    ):
        return read_part(
            queries_in,
            keys_in,
            values_in,
            key_part,
            value_part,
            out_part,
            gain_part,
            memory_part,
            segment,
            seg_length,
        )

    result, read_back = jax.vjp(
        reading,
        queries,
        seg_keys,
        seg_values,
        key_weight,
        value_weight,
        out_weight,
        norm_gain,
        memory_in,
    )
    valid_rows = (jnp.arange(segment.shape[0]) < seg_length)[:, None]
    d_result = cotangent[0, 0].astype(jnp.float32) * valid_rows
    d_queries, d_keys_read, d_values_read, key_read, value_read, out_read, gain_read, d_memory = (
        read_back(d_result)
    )
    later_keep, later_grad = entering((retain, d_memory), CHAIN, compose, identity, True)
    d_retain = jnp.sum(later_grad * (memory_in - written), axis=1)
    d_written = (1.0 - retain)[:, None] * later_grad
    d_keys_write, d_values_write, query_write, out_write, gain_write, gate_grad, start_grad = (
        write_back((d_retain, d_written))
    )
    d_keys = (d_keys_read.astype(jnp.float32) + d_keys_write.astype(jnp.float32)).astype(
        jnp.bfloat16
    )
    d_values = (d_values_read.astype(jnp.float32) + d_values_write.astype(jnp.float32)).astype(
        jnp.bfloat16
    )
    query_prep, key_prep, value_prep, gain_prep = prep_back((d_queries, d_keys, d_values))
    query_total = query_write.astype(jnp.float32) + query_prep.astype(jnp.float32)
    gain_total = gain_read + gain_write + gain_prep
    start_total = start_grad + prefix_keep[:, None] * d_memory
    key_total = key_read.astype(jnp.float32) + key_prep.astype(jnp.float32)
    value_total = value_read.astype(jnp.float32) + value_prep.astype(jnp.float32)
    out_total = out_read.astype(jnp.float32) + out_write.astype(jnp.float32)
    grad_query, grad_key, grad_value, grad_out, grad_gain, grad_gate, grad_memory = (
        lax.psum_scatter(query_total, CHAIN_DP, scatter_dimension=0, tiled=True),
        lax.psum_scatter(key_total, CHAIN_DP, scatter_dimension=0, tiled=True),
        lax.psum_scatter(value_total, CHAIN_DP, scatter_dimension=0, tiled=True),
        lax.psum_scatter(out_total, CHAIN_DP, scatter_dimension=0, tiled=True),
        lax.psum_scatter(gain_total, CHAIN_DP, scatter_dimension=0, tiled=True),
        lax.psum_scatter(gate_grad, CHAIN_DP, scatter_dimension=0, tiled=True),
        lax.psum_scatter(start_total, CHAIN_DP, scatter_dimension=1, tiled=True),
    )
    layer_output = result.astype(jnp.bfloat16)[None, None]
    return (
        layer_output,
        grad_query,
        grad_key,
        grad_value,
        grad_out,
        grad_gain,
        grad_gate,
        grad_memory,
    )


def solution(mesh):
    split = Mesh(
        mesh.devices.reshape(4, 4, 2, mesh.shape["dp"]), ("chain_0", "chain_1", "chain_2", "dp")
    )
    placed = (
        P("dp", CHAIN, None, None),
        P("dp", CHAIN),
        P(),
        P(),
        P(),
        P(),
        P(),
        P(),
        P(),
        P(),
        P("dp", CHAIN, None, None),
    )
    return jax.shard_map(
        per_device,
        mesh=split,
        in_specs=placed,
        out_specs=(
            P("dp", CHAIN, None, None),
            P(CHAIN_DP, None),
            P(CHAIN_DP, None),
            P(CHAIN_DP, None),
            P(CHAIN_DP, None),
            P(CHAIN_DP),
            P(CHAIN_DP),
            P(None, CHAIN_DP),
        ),
        check_vma=False,
    )
```

profile of v0, /device:TPU:32, one launch (start us, length us, event | category | flops | bytes accessed | tf_op | source)
XLA Modules:
  0.0 573.9 jit_solution(10842302888583122627)
XLA Ops:
  10.8 1.4 convolution_convert_fusion.20
  12.2 1.4 convolution_convert_fusion.21
  15.9 1.3 bitcast_reduce_fusion
  21.6 1.8 all-gather.4
  23.4 9.7 %all-gather.5 = f32[4,1,128]{2,1,0:T(1,128)S(1)} all-gather(f32[1,1,128]{2,1,0:T(1,128)S(1)} %multiply_bitcast_fusion), channel_id=5, replica_groups=mesh['chain_0'=4,'chain_1'=4,'chain_2'=2,'dp'=8] {'chain_1'}, dimensions={0}, use_global_device_ids=true | all-gather | bytes 2560 | tf_op jit(solution)/shard_map/all_gather | solution.py:27
  34.3 4.4 all-gather.23.cloned.1.call-done
  38.6 2.1 bitcast_add_fusion.10
  41.4 34.1 %all-gather.15.cloned.1.call-done = f32[4,128,1024]{2,1,0:T(8,128)} async-done(((f32[1,128,1024]{2,1,0:T(8,128)}), f32[4,128,1024]{2,1,0:T(8,128)}) %all-gather.15.cloned.1.call-update) | async-done | bytes 2097168 | tf_op jit(solution)/shard_map/all_gather | solution.py:27
  75.5 2.5 multiply_add_fusion.2
  78.2 3.2 convolution_convert_fusion.14
  81.4 1.8 copy.61
  83.2 2.2 fusion.18
  85.4 1.8 copy.59
  87.7 8.3 %all-gather.6 = f32[4,1,128]{2,1,0:T(1,128)S(1)} all-gather(f32[1,1,128]{2,1,0:T(1,128)S(1)} %get-tuple-element.61), channel_id=1, replica_groups=mesh['chain_0'=4,'chain_1'=4,'chain_2'=2,'dp'=8] {'chain_0'}, dimensions={0}, use_global_device_ids=true | all-gather | bytes 2560 | tf_op jit(solution)/shard_map/all_gather | solution.py:27
  98.5 29.1 %all-gather.17.cloned.1.call-done = f32[4,128,1024]{2,1,0:T(8,128)} async-done(((f32[1,128,1024]{2,1,0:T(8,128)}), f32[4,128,1024]{2,1,0:T(8,128)}) %all-gather.17.cloned.1.call-update) | async-done | bytes 2097168 | tf_op jit(solution)/shard_map/all_gather | solution.py:27
  127.6 3.5 multiply_reduce_fusion.3
  134.4 1.7 copy.58
  136.0 1.5 pad_maximum_fusion
  137.6 1.6 copy.57
  139.2 1.6 fusion.6
  146.8 14.7 %all-gather.25.cloned.1.call-done = f32[256,1024]{1,0:T(8,128)} async-done(((f32[128,1024]{1,0:T(8,128)}), f32[256,1024]{1,0:T(8,128)}) %all-gather.25.cloned.1.call-update) | async-done | bytes 1048592 | tf_op jit(solution)/shard_map/all_gather | solution.py:27
  161.5 2.1 bitcast_add_fusion.4
  163.7 34.7 %all-gather.19.cloned.1.call-done = f32[4,128,1024]{2,1,0:T(8,128)} async-done(((f32[1,128,1024]{2,1,0:T(8,128)}), f32[4,128,1024]{2,1,0:T(8,128)}) %all-gather.19.cloned.1.call-update) | async-done | bytes 2097168 | tf_op jit(solution)/shard_map/all_gather | solution.py:27
  198.4 2.5 multiply_add_fusion.1
  201.1 8.7 %all-gather.7 = f32[4,1,128]{2,1,0:T(1,128)S(1)} all-gather(f32[1,1,128]{2,1,0:T(1,128)} %get-tuple-element.60), channel_id=1, replica_groups=mesh['chain_0'=4,'chain_1'=4,'chain_2'=2,'dp'=8] {'chain_0'}, dimensions={0}, use_global_device_ids=true | all-gather | bytes 2560 | tf_op jit(solution)/shard_map/all_gather | solution.py:27
  210.4 1.3 multiply_divide_fusion
  211.7 2.3 fusion.10
  214.0 2.3 fusion.13
  217.4 2.1 fusion.71
  219.6 1.5 fusion.16
  221.1 29.4 %all-gather.21.cloned.1.call-done = f32[4,128,1024]{2,1,0:T(8,128)} async-done(((f32[1,128,1024]{2,1,0:T(8,128)}), f32[4,128,1024]{2,1,0:T(8,128)}) %all-gather.21.cloned.1.call-update) | async-done | bytes 2097168 | tf_op jit(solution)/shard_map/all_gather | solution.py:27
  250.6 3.9 multiply_reduce_fusion.1
  255.3 1.5 convolution_convert_fusion.11
  256.9 1.8 copy.64
  258.6 1.4 fusion.43
  260.1 1.4 fusion.54
  265.2 2.8 convert_add_fusion
  269.4 1.4 fusion.9
  270.8 1.4 fusion.12
  272.2 2.8 convert_add_fusion.1
  275.9 2.8 fusion.22
  278.8 1.9 fusion.138
  281.8 78.2 %all-reduce.8 = (f32[1024]{0:T(1024)S(1)}, f32[1024]{0:T(1024)S(1)}) all-reduce(f32[1024]{0:T(1024)S(1)} %add_add_fusion.2, f32[1024]{0:T(1024)S(1)} %bitcast.563), channel_id=10, replica_groups=mesh['chain_0'=4,'chain_1'=4,'chain_2'=2,'dp'=8] {'chain_0','chain_1','c..., use_global_device_ids=true, to_apply=%region_18.19.clone | all-reduce | flops 2048 | bytes 16384
  361.2 198.9 %all-reduce.12.cloned.1.call-done = (f32[1024,1024]{1,0:T(8,128)}, f32[1024,256]{1,0:T(8,128)}, f32[1024,256]{1,0:T(8,128)}, f32[1024,1024]{1,0:T(8,128)}, f32[128,1024]{1,0:T(8,128)}) async-done(((f32[1024,1024]{1,0:T(8,128)}, f32[1024,256]{1,0:T(8,128)}, f32[1024,256]{1,0:T(8,128)}, f32[1024,1024]{1,0:T(8,128)}, f32[128,1024]{1,0:T(8,128)}), (f32[1024,1024]{1,0:T(8,128)}, f32[1024,256]{1,0:T(8,128)}, ...) | async-done | bytes 11010064
  560.1 1.4 constant_dynamic-slice_fusion.4
  561.5 1.3 constant_dynamic-slice_fusion.3
  562.8 1.3 constant_dynamic-slice_fusion.2
  564.1 1.4 constant_dynamic-slice_fusion.1
  (295 shorter events, 35.1 us)
Async XLA Ops:
  7.2 7.4 %copy-start = (bf16[1024,1024]{1,0:T(8,128)(2,1)S(1)}, bf16[1024,1024]{1,0:T(8,128)(2,1)}, u32[]{:S(2)}) copy-start(bf16[1024,1024]{1,0:T(8,128)(2,1)} %param.13) | copy-start | bytes 6291460
  7.2 7.4 %copy-start.7 = (bf16[128,1024]{1,0:T(8,128)(2,1)S(1)}, bf16[128,1024]{1,0:T(8,128)(2,1)}, u32[]{:S(2)}) copy-start(bf16[128,1024]{1,0:T(8,128)(2,1)} %param.20) | copy-start | bytes 786436
  7.2 7.4 %copy-start.43 = (f32[1024]{0:T(1024)S(1)}, f32[1024]{0:T(1024)}, u32[]{:S(2)}) copy-start(f32[1024]{0:T(1024)} %param.17) | copy-start | bytes 12292
  7.2 31.4 %all-gather.23.cloned.1.call-start = ((), (), s32[]{:S(2)}) async-start(), calls=%async_computation.4 | async-start | bytes 1572864 | tf_op jit(solution)/shard_map/all_gather | solution.py:27
  9.1 5.9 %copy-start.74 = (f32[128]{0:T(128)}, f32[128]{0:T(128)S(1)}, u32[]{:S(2)}) copy-start(f32[128]{0:T(128)S(1)} %fusion.123) | copy-start | bytes 1540
  10.8 5.1 copy-start.76
  20.0 13.0 %copy-start.104 = (f32[128]{0:T(128)}, f32[128]{0:T(128)S(1)}, u32[]{:S(2)}) copy-start(f32[128]{0:T(128)S(1)} %get-tuple-element.78) | copy-start | bytes 1540
  21.5 54.0 %all-gather.15.cloned.1.call-start = ((), (), s32[]{:S(2)}) async-start(), calls=%async_computation | async-start | bytes 2621440 | tf_op jit(solution)/shard_map/all_gather | solution.py:27
  23.4 54.7 %copy-start.65 = (f32[2,1,128]{2,1,0:T(1,128)}, f32[2,1,128]{2,1,0:T(1,128)S(1)}, u32[]{:S(2)}) copy-start(f32[2,1,128]{2,1,0:T(1,128)S(1)} %all-gather.4) | copy-start | bytes 3076
  33.7 7.1 %copy-start.84 = (f32[128]{0:T(128)}, f32[128]{0:T(128)S(1)}, u32[]{:S(2)}) copy-start(f32[128]{0:T(128)S(1)} %get-tuple-element.74) | copy-start | bytes 1540
  34.3 6.5 %copy-start.82 = (f32[128]{0:T(128)}, f32[128]{0:T(128)S(1)}, u32[]{:S(2)}) copy-start(f32[128]{0:T(128)S(1)} %get-tuple-element.72) | copy-start | bytes 1540
  34.3 41.3 %copy-start.81 = (f32[128]{0:T(128)}, f32[128]{0:T(128)S(1)}, u32[]{:S(2)}) copy-start(f32[128]{0:T(128)S(1)} %get-tuple-element.63) | copy-start | bytes 1540
  40.8 37.4 %copy-start.99 = (f32[128]{0:T(128)S(1)}, f32[128]{0:T(128)}, u32[]{:S(2)}) copy-start(f32[128]{0:T(128)} %get-tuple-element.87) | copy-start | bytes 1540
  40.8 86.8 %all-gather.17.cloned.1.call-start = ((), (), s32[]{:S(2)}) async-start(), calls=%async_computation.1 | async-start | bytes 2621440 | tf_op jit(solution)/shard_map/all_gather | solution.py:27
  41.4 36.8 %copy-start.86 = (f32[128]{0:T(128)}, f32[128]{0:T(128)S(1)}, u32[]{:S(2)}) copy-start(f32[128]{0:T(128)S(1)} %get-tuple-element.67) | copy-start | bytes 1540
  41.4 86.2 %copy-start.61 = (f32[128]{0:T(128)}, f32[128]{0:T(128)S(1)}, u32[]{:S(2)}) copy-start(f32[128]{0:T(128)S(1)} %get-tuple-element.65) | copy-start | bytes 1540
  41.4 86.2 %copy-start.63 = (f32[128]{0:T(128)}, f32[128]{0:T(128)S(1)}, u32[]{:S(2)}) copy-start(f32[128]{0:T(128)S(1)} %get-tuple-element.66) | copy-start | bytes 1540
  78.1 5.1 copy-start.72
  78.1 83.4 %all-gather.25.cloned.1.call-start = ((), (), s32[]{:S(2)}) async-start(), calls=%async_computation.5 | async-start | bytes 1572864 | tf_op jit(solution)/shard_map/all_gather | solution.py:27
  81.4 14.6 %copy-start.77 = (pred[128]{0:T(512)(128)(4,1)S(1)}, pred[128]{0:T(512)(128)(4,1)}, u32[]{:S(2)}) copy-start(pred[128]{0:T(512)(128)(4,1)} %copy-done.76) | copy-start | bytes 388
  98.5 32.7 %copy-start.91 = (f32[128]{0:T(128)}, f32[128]{0:T(128)S(1)}, u32[]{:S(2)}) copy-start(f32[128]{0:T(128)S(1)} %get-tuple-element.49) | copy-start | bytes 1540
  127.6 5.2 copy-start.29
  131.2 9.5 %copy-start.106 = (f32[128]{0:T(128)}, f32[128]{0:T(128)S(1)}, u32[]{:S(2)}) copy-start(f32[128]{0:T(128)S(1)} %get-tuple-element.47) | copy-start | bytes 1540
  131.3 7.9 %copy-start.87 = (f32[128]{0:T(128)}, f32[128]{0:T(128)S(1)}, u32[]{:S(2)}) copy-start(f32[128]{0:T(128)S(1)} %fusion.124) | copy-start | bytes 1540
  146.7 51.7 %all-gather.19.cloned.1.call-start = ((), (), s32[]{:S(2)}) async-start(), calls=%async_computation.2 | async-start | bytes 2621440 | tf_op jit(solution)/shard_map/all_gather | solution.py:27
  163.7 86.8 %all-gather.21.cloned.1.call-start = ((), (), s32[]{:S(2)}) async-start(), calls=%async_computation.3 | async-start | bytes 2621440 | tf_op jit(solution)/shard_map/all_gather | solution.py:27
  201.0 359.1 %all-reduce.12.cloned.1.call-start = ((), (), s32[]{:S(2)}) async-start(), calls=%async_computation.6 | async-start | bytes 22020096
  201.0 15.3 %copy-start.21 = (bf16[4,4,128,256]{2,3,1,0:T(8,128)(2,1)S(1)}, bf16[4,4,128,256]{2,3,1,0:T(8,128)(2,1)}, u32[]{:S(2)}) copy-start(bf16[4,4,128,256]{2,3,1,0:T(8,128)(2,1)} %copy-done.20) | copy-start | bytes 3145732
  201.0 15.2 %copy-start.42 = (bf16[256,256]{0,1:T(8,128)(2,1)S(1)}, bf16[256,256]{0,1:T(8,128)(2,1)}, u32[]{:S(2)}) copy-start(bf16[256,256]{0,1:T(8,128)(2,1)} %copy.57) | copy-start | bytes 393220
  211.7 5.7 copy-start.35
  211.7 5.7 copy-start.100
  219.5 31.0 %copy-start.62 = (f32[128]{0:T(128)S(1)}, f32[128]{0:T(128)}, u32[]{:S(2)}) copy-start(f32[128]{0:T(128)} %copy-done.61) | copy-start | bytes 1540
  219.5 31.0 %copy-start.64 = (f32[128]{0:T(128)S(1)}, f32[128]{0:T(128)}, u32[]{:S(2)}) copy-start(f32[128]{0:T(128)} %copy-done.63) | copy-start | bytes 1540
  219.5 31.0 %copy-start.79 = (f32[128]{0:T(128)S(1)}, f32[128]{0:T(128)}, u32[]{:S(2)}) copy-start(f32[128]{0:T(128)} %get-tuple-element.62) | copy-start | bytes 1540
  219.5 31.0 %copy-start.80 = (f32[128]{0:T(128)S(1)}, f32[128]{0:T(128)}, u32[]{:S(2)}) copy-start(f32[128]{0:T(128)} %get-tuple-element.71) | copy-start | bytes 1540
  219.5 31.0 %copy-start.83 = (f32[128]{0:T(128)S(1)}, f32[128]{0:T(128)}, u32[]{:S(2)}) copy-start(f32[128]{0:T(128)} %get-tuple-element.73) | copy-start | bytes 1540
  219.6 31.0 %copy-start.85 = (f32[128]{0:T(128)S(1)}, f32[128]{0:T(128)}, u32[]{:S(2)}) copy-start(f32[128]{0:T(128)} %get-tuple-element.64) | copy-start | bytes 1540
  219.6 31.0 %copy-start.93 = (f32[128]{0:T(128)S(1)}, f32[128]{0:T(128)}, u32[]{:S(2)}) copy-start(f32[128]{0:T(128)} %get-tuple-element.45) | copy-start | bytes 1540
  219.6 31.0 %copy-start.94 = (f32[128]{0:T(128)S(1)}, f32[128]{0:T(128)}, u32[]{:S(2)}) copy-start(f32[128]{0:T(128)} %get-tuple-element.46) | copy-start | bytes 1540
  219.6 31.0 %copy-start.95 = (f32[128]{0:T(128)S(1)}, f32[128]{0:T(128)}, u32[]{:S(2)}) copy-start(f32[128]{0:T(128)} %get-tuple-element.56) | copy-start | bytes 1540
  219.6 31.0 %copy-start.96 = (f32[128]{0:T(128)S(1)}, f32[128]{0:T(128)}, u32[]{:S(2)}) copy-start(f32[128]{0:T(128)} %get-tuple-element.57) | copy-start | bytes 1540
  219.6 31.0 %copy-start.97 = (f32[128]{0:T(128)S(1)}, f32[128]{0:T(128)}, u32[]{:S(2)}) copy-start(f32[128]{0:T(128)} %get-tuple-element.58) | copy-start | bytes 1540
  219.6 31.0 %copy-start.98 = (f32[128]{0:T(128)S(1)}, f32[128]{0:T(128)}, u32[]{:S(2)}) copy-start(f32[128]{0:T(128)} %get-tuple-element.59) | copy-start | bytes 1540
  250.6 4.7 copy-start.2
  250.6 4.7 copy-start.69
  255.3 4.7 copy-start.38
  260.1 8.9 %copy-start.44 = (bf16[128,4,64]{0,2,1:T(8,128)(2,1)}, bf16[128,4,64]{0,2,1:T(8,128)(2,1)S(1)}, u32[]{:S(2)}) copy-start(bf16[128,4,64]{0,2,1:T(8,128)(2,1)S(1)} %fusion.43) | copy-start | bytes 196612
  275.9 4.7 copy-start.16
  (69 other events, 137.1 us)
Sparse Core Ops, SparseCore 0:
  21.6 16.9 all-gather.22
  40.9 34.5 all-gather.14
  78.2 49.3 all-gather.16
  146.8 14.6 all-gather.24
  163.8 34.5 all-gather.18
  201.1 49.3 all-gather.20
  275.1 284.9 all-reduce.11
where the time goes:
time: 578 us; the launch traced here: 574 us
  waiting for transfers between devices  345 us (60%)
  blocking collectives  107 us (19%)
  matrix products  46.5 us (8%)
  other arithmetic  30.1 us (5%)
  local copies, waits for them, and re-layouts  28.4 us (5%)
  between operations  16.3 us (3%)
    unnamed x8, waiting for transfers between devices  199 us
    all_gather x6, waiting for transfers between devices, entering(): pieces = jax.tree.map(lambda part: lax.all_gather(part, axis), subtotal)  146 us
    unnamed x1, blocking collectives  78.2 us
    all_gather x4, blocking collectives, entering(): pieces = jax.tree.map(lambda part: lax.all_gather(part, axis), subtotal)  28.6 us
    unnamed x228, local copies, waits for them, and re-layouts  16.3 us
  transfers between devices with their start and end apart: 7, of which 7 were waited for; matrix products, arithmetic and copies ran while one was open for 5% of the time, Pallas kernels for 0%

commit v1 on v0

--- a/solution.py
+++ b/solution.py
@@ -1,37 +1,356 @@
+import functools
+
 import jax
 import jax.numpy as jnp
 from jax import lax
+from jax.experimental import pallas as pl
+from jax.experimental.pallas import tpu as pltpu
 from jax.sharding import Mesh
 from jax.sharding import PartitionSpec as P
 
 HEAD = 64
-CHAIN = ("chain_0", "chain_1", "chain_2")
-CHAIN_DP = ("chain_0", "chain_1", "chain_2", "dp")
+AXES = ("zl", "x", "c", "zh", "y")
+MESH = pl.DeviceIdType.MESH
+VMEM_SPEC = pl.BlockSpec(memory_space=pltpu.VMEM)
+
+
+def z_shift(step):
+    place = lax.rem(lax.axis_index("zh") * 4 + lax.axis_index("zl") + step, 8)
+    return {"zh": lax.div(place, 4), "zl": lax.rem(place, 4)}
+
+
+def shift(axis, step):
+    if axis == "z":
+        return z_shift(step % 8)
+    return {axis: lax.rem(lax.axis_index(axis) + step % 4, 4)}
+
+
+def place_of(axis):
+    return lax.axis_index("zl" if axis == "z" else axis)
+
+
+def remote(source, target, send, receive, device):
+    return pltpu.make_async_remote_copy(
+        src_ref=source,
+        dst_ref=target,
+        send_sem=send,
+        recv_sem=receive,
+        device_id=device,
+        device_id_type=MESH,
+    )
+
+
+def greet(devices):
+    barrier = pltpu.get_barrier_semaphore()
+    for device in devices:
+        pl.semaphore_signal(barrier, inc=1, device_id=device, device_id_type=MESH)
+    pl.semaphore_wait(barrier, len(devices))
+
+
+class Ring:
+    def __init__(self, axis, work, landing, out, send, receive):
+        self.work, self.landing, self.out = work, landing, out
+        self.send, self.receive = send, receive
+        self.me = place_of(axis)
+        self.up, self.down = shift(axis, 1), shift(axis, -1)
+        self.copies = []
+
+    def at(self, step):
+        return lax.rem(self.me + step, 4)
+
+    def push(self, half, step, device):
+        slot = len(self.copies)
+        copy = remote(
+            self.work.at[half, self.at(step)],
+            self.landing.at[slot],
+            self.send.at[slot],
+            self.receive.at[slot],
+            device,
+        )
+        copy.start()
+        self.copies.append(copy)
+
+    def first(self):
+        self.push(0, 2, self.up)
+        self.push(1, 2, self.down)
+        self.push(1, 1, self.up)
+        self.push(0, 3, self.down)
+
+    def second(self):
+        for half, step, device in ((0, 1, self.up), (1, 3, self.down)):
+            self.copies[half].wait_recv()
+            self.work[half, self.at(step)] += self.landing[half]
+            self.push(half, step, device)
+
+    def finish(self):
+        for slot in range(2, 6):
+            self.copies[slot].wait_recv()
+        self.out[0] = self.work[0, self.me] + self.landing[3] + self.landing[4]
+        self.out[1] = self.work[1, self.me] + self.landing[2] + self.landing[5]
+
+    def drain(self):
+        for copy in self.copies:
+            copy.wait_send()
+
+
+ORDERS = (("x", "y", "z"), ("y", "z", "x"), ("z", "x", "y"))
+WIDTHS = ((1024,), (1024,), (256, 256, 256))
+TOTAL = 2816
+
+
+def sum_kernel(*refs):
+    inputs, refs = refs[:5], refs[5:]
+    out_ref, refs = refs[0], refs[1:]
+    landed, refs = refs[:5], refs[5:]
+    works, refs = refs[:3], refs[3:]
+    rings_of, refs = refs[:18], refs[18:]
+    sent, mate, fold_in, core_send, core_receive, ring_send, ring_receive, fold_sems = refs
+    core = lax.axis_index("c")
+    other = {"c": 1 - core}
+    far = z_shift(4)
+    greet(
+        [other, far]
+        + [shift(axis, step) for axis in ("x", "y", "z") for step in (1, -1)]
+    )
+    core_copies = []
+    for k in range(5):
+        copy = remote(
+            inputs[k].at[:, 1 - core], landed[k], core_send.at[k], core_receive.at[k], other
+        )
+        copy.start()
+        core_copies.append(copy)
+    rings = []
+    k = 0
+    for part in range(3):
+        order = ORDERS[part]
+        work = works[part]
+        half_width = sum(WIDTHS[part]) // 2
+        members = []
+        start = 0
+        for width in WIDTHS[part]:
+            members.append((k, width, start))
+            core_copies[k].wait_recv()
+            k += 1
+            start += width
+
+        def build(zl, carry, members=members, order=order, work=work, half_width=half_width):
+            for x in range(4):
+                block = zl * 4 + x
+                for member, width, start in members:
+                    for col in range(0, width, 128):
+                        cols = pl.ds(col, 128)
+                        half = (start + col) // half_width
+                        to = pl.ds((start + col) % half_width, 128)
+                        rows = (
+                            inputs[member][block, core, :, cols] + landed[member][block, :, cols]
+                        )
+                        low = lax.broadcasted_iota(jnp.int32, (8, 128), 0) < 4
+                        for pair in range(2):
+                            a = rows[pair * 8 : pair * 8 + 8]
+                            b = rows[16 + pair * 8 : 24 + pair * 8]
+                            tiles = (
+                                jnp.where(low, a, pltpu.roll(b, 4, 0)),
+                                jnp.where(low, pltpu.roll(a, 4, 0), b),
+                            )
+                            for bit in range(2):
+                                where = {"z": zl, "x": x, "y": pair * 2 + bit}
+                                index = (half,) + tuple(where[axis] for axis in order)
+                                work[index + (slice(None), to)] = tiles[bit]
+            return carry
+
+        lax.fori_loop(0, 4, build, 0)
+        stages = []
+        for stage in range(3):
+            n = part * 3 + stage
+            stages.append(
+                Ring(
+                    order[stage],
+                    work if stage == 0 else rings_of[2 * (n - 1) + 1],
+                    rings_of[2 * n],
+                    rings_of[2 * n + 1],
+                    ring_send.at[n],
+                    ring_receive.at[n],
+                )
+            )
+        rings.append(stages)
+        stages[0].first()
+    for stage in range(3):
+        for part in range(3):
+            rings[part][stage].second()
+        for part in range(3):
+            rings[part][stage].finish()
+            if stage < 2:
+                rings[part][stage + 1].first()
+    total = jnp.concatenate(
+        [rings_of[2 * (part * 3 + 2) + 1][half] for part in range(3) for half in range(2)], axis=1
+    )
+    turned = pltpu.roll(total, 4, 0)
+    high = lax.axis_index("zh")
+    fold = lax.broadcasted_iota(jnp.int32, (8, TOTAL // 2), 0) < 4
+
+    def folded(upright, upside):
+        return jnp.where(fold, upright[:, : TOTAL // 2], upside[:, TOTAL // 2 :])
+
+    straight, crossed = folded(total, turned), folded(turned, total)
+    sent[...] = jnp.where(high == 1, straight, crossed)
+    mate[...] = jnp.where(high == 0, straight, crossed)
+    last = remote(sent, fold_in, fold_sems.at[0], fold_sems.at[1], far)
+    last.start()
+    for copy in core_copies:
+        copy.wait_send()
+    for stages in rings:
+        for ring in stages:
+            ring.drain()
+    last.wait()
+    out_ref[...] = mate[...] + fold_in[...]
+
+
+def sum_over_devices(*arrays):
+    f32 = jnp.float32
+    scratch = [pltpu.VMEM((16, 32, a.shape[1]), f32) for a in arrays]
+    halves = [sum(widths) // 2 for widths in WIDTHS]
+    scratch += [pltpu.VMEM((2, 4, 4, 4, 8, n), f32) for n in halves]
+    for n in halves:
+        for stage in range(3):
+            rest = (4,) * (2 - stage) + (8, n)
+            scratch += [pltpu.VMEM((6,) + rest, f32), pltpu.VMEM((2,) + rest, f32)]
+    scratch += [pltpu.VMEM((8, TOTAL // 2), f32)] * 3
+    scratch += [
+        pltpu.SemaphoreType.DMA((5,)),
+        pltpu.SemaphoreType.DMA((5,)),
+        pltpu.SemaphoreType.DMA((9, 6)),
+        pltpu.SemaphoreType.DMA((9, 6)),
+        pltpu.SemaphoreType.DMA((2,)),
+    ]
+    out = pl.pallas_call(
+        sum_kernel,
+        out_shape=jax.ShapeDtypeStruct((8, TOTAL // 2), f32),
+        in_specs=[VMEM_SPEC] * 5,
+        out_specs=VMEM_SPEC,
+        scratch_shapes=scratch,
+        compiler_params=pltpu.CompilerParams(
+            collective_id=2, has_side_effects=True, vmem_limit_bytes=60 << 20
+        ),
+        name="sum_over_devices",
+    )(*[a.reshape(16, 2, 32, a.shape[1]) for a in arrays])
+    return jnp.concatenate([out[:4], out[4:]], axis=1)
+
+
+WIDE = 1152
+
+
+def joined(earlier, later):
+    keep = later[:, 1024:]
+    gain = jnp.concatenate([keep] * 9, axis=1)
+    added = jnp.concatenate([later[:, :1024], jnp.zeros_like(keep)], axis=1)
+    return gain * earlier + added
+
+
+def identity_rows(rows):
+    return jnp.concatenate(
+        [jnp.zeros((rows, 1024), jnp.float32), jnp.ones((rows, 128), jnp.float32)], axis=1
+    )
+
+
+def scan_kernel(reverse, add_ref, keep_ref, out_ref, own, mate, pair, xs, zs, backs, down, up, far, send, receive):
+    core, x, zl = lax.axis_index("c"), lax.axis_index("x"), lax.axis_index("zl")
+    other = {"c": 1 - core}
+    x_peers = [{"x": lax.rem(x + k, 4)} for k in (1, 2, 3)]
+    z_peers = [{"zl": lax.rem(zl + k, 4)} for k in (1, 2, 3)]
+    own[:, :1024] = add_ref[...]
+    own[:, 1024:] = keep_ref[...]
+    greet([other] + x_peers + z_peers)
+
+    def rows_of(start, count):
+        return pl.ds(pl.multiple_of(start, count), count)
+
+    mine = rows_of(core * 64, 64)
+    theirs = rows_of((1 - core) * 64, 64)
+    copies = []
+
+    def push(source, target, device):
+        n = len(copies)
+        copy = remote(source, target, send.at[n], receive.at[n], device)
+        copy.start()
+        copies.append(copy)
+        return copy
+
+    push(own.at[theirs], mate, other).wait_recv()
+    leads = core == (1 if reverse else 0)
+    kept, got = own[mine], mate[...]
+    earlier = jnp.where(leads, kept, got)
+    pair[...] = joined(earlier, jnp.where(leads, got, kept))
+    started = [
+        push(pair.at[rows_of(lax.rem(x + k, 4) * 16, 16)], xs.at[x], x_peers[k - 1])
+        for k in (1, 2, 3)
+    ]
+    xs[x] = pair[rows_of(x * 16, 16)]
+    for copy in started:
+        copy.wait_recv()
+    order = (3, 2, 1, 0) if reverse else (0, 1, 2, 3)
+    inside = {}
+    running = None
+    for k in order:
+        inside[k] = running
+        running = xs[k] if running is None else joined(running, xs[k])
+    zs[zl] = running
+    started = [push(zs.at[zl], zs.at[zl], z_peers[k - 1]) for k in (1, 2, 3)]
+    for copy in started:
+        copy.wait_recv()
+    before = identity_rows(16)
+    for k in order[:3]:
+        passed = k > zl if reverse else k < zl
+        before = jnp.where(passed, joined(before, zs[k]), before)
+    for k in order:
+        backs[k] = before if inside[k] is None else joined(before, inside[k])
+    started = [
+        push(backs.at[lax.rem(x + k, 4)], down.at[rows_of(x * 16, 16)], x_peers[k - 1])
+        for k in (1, 2, 3)
+    ]
+    down[rows_of(x * 16, 16)] = backs[x]
+    for copy in started:
+        copy.wait_recv()
+    lead = down[...]
+    follow = joined(lead, earlier)
+    up[...] = jnp.where(leads, follow, lead)
+    last = push(up, far, other)
+    out_ref[mine] = jnp.where(leads, lead, follow)
+    last.wait_recv()
+    out_ref[theirs] = far[...]
+    for copy in copies:
+        copy.wait_send()
+
+
+def entering(keep, added, reverse):
+    f32 = jnp.float32
+    out = pl.pallas_call(
+        functools.partial(scan_kernel, reverse),
+        out_shape=jax.ShapeDtypeStruct((128, WIDE), f32),
+        in_specs=[VMEM_SPEC] * 2,
+        out_specs=VMEM_SPEC,
+        scratch_shapes=[
+            pltpu.VMEM((128, WIDE), f32),
+            pltpu.VMEM((64, WIDE), f32),
+            pltpu.VMEM((64, WIDE), f32),
+            pltpu.VMEM((4, 16, WIDE), f32),
+            pltpu.VMEM((4, 16, WIDE), f32),
+            pltpu.VMEM((4, 16, WIDE), f32),
+            pltpu.VMEM((64, WIDE), f32),
+            pltpu.VMEM((64, WIDE), f32),
+            pltpu.VMEM((64, WIDE), f32),
+            pltpu.SemaphoreType.DMA((11,)),
+            pltpu.SemaphoreType.DMA((11,)),
+        ],
+        compiler_params=pltpu.CompilerParams(
+            collective_id=1 if reverse else 0, has_side_effects=True
+        ),
+        name="suffix" if reverse else "prefix",
+    )(added, jnp.broadcast_to(keep[:, None], (128, 128)))
+    return out[:, 1024], out[:, :1024]
 
 
 epsilon = 1e-05
 score_scale = 0.125
-
-
-def filled_with(shard, identity):
-    return jax.tree.map(
-        lambda a, e: jnp.broadcast_to(jnp.asarray(e, a.dtype), a.shape), shard, identity
-    )
-
-
-def entering(shard, axes, combine, identity, reverse):
-    before = start = filled_with(shard, identity)
-    subtotal = shard
-    for axis in reversed(axes):
-        peers, place = (lax.axis_size(axis), lax.axis_index(axis))
-        pieces = jax.tree.map(lambda part: lax.all_gather(part, axis), subtotal)
-        inside, subtotal = (start, start)
-        for k in reversed(range(peers)) if reverse else range(peers):
-            passed = k > place if reverse else k < place
-            subtotal = combine(subtotal, jax.tree.map(lambda part: part[k], pieces))
-            inside = jax.tree.map(lambda new, old: jnp.where(passed, new, old), subtotal, inside)
-        before = combine(inside, before)
-    return before
 
 
 def normalize(activations, norm_gain):
@@ -126,12 +445,6 @@
     return (retain, written)
 
 
-def compose(earlier, later):
-    keep_early, add_early = earlier
-    keep_later, add_later = later
-    return (keep_early * keep_later, keep_later[:, None] * add_early + add_later)
-
-
 def per_device(
     segments,
     lengths,
@@ -179,10 +492,7 @@
         gate_vector,
         memory_start,
     )
-    identity = (jnp.ones_like(retain), jnp.zeros_like(written))
-    prefix_keep, prefix_add = entering(
-        (retain, (1.0 - retain)[:, None] * written), CHAIN, compose, identity, False
-    )
+    prefix_keep, prefix_add = entering(retain, (1.0 - retain)[:, None] * written, False)
     memory_in = prefix_keep[:, None] * memory_start + prefix_add
 
     def reading(
@@ -217,7 +527,7 @@
     d_queries, d_keys_read, d_values_read, key_read, value_read, out_read, gain_read, d_memory = (
         read_back(d_result)
     )
-    later_keep, later_grad = entering((retain, d_memory), CHAIN, compose, identity, True)
+    later_keep, later_grad = entering(retain, d_memory, True)
     d_retain = jnp.sum(later_grad * (memory_in - written), axis=1)
     d_written = (1.0 - retain)[:, None] * later_grad
     d_keys_write, d_values_write, query_write, out_write, gain_write, gate_grad, start_grad = (
@@ -236,15 +546,14 @@
     key_total = key_read.astype(jnp.float32) + key_prep.astype(jnp.float32)
     value_total = value_read.astype(jnp.float32) + value_prep.astype(jnp.float32)
     out_total = out_read.astype(jnp.float32) + out_write.astype(jnp.float32)
-    grad_query, grad_key, grad_value, grad_out, grad_gain, grad_gate, grad_memory = (
-        lax.psum_scatter(query_total, CHAIN_DP, scatter_dimension=0, tiled=True),
-        lax.psum_scatter(key_total, CHAIN_DP, scatter_dimension=0, tiled=True),
-        lax.psum_scatter(value_total, CHAIN_DP, scatter_dimension=0, tiled=True),
-        lax.psum_scatter(out_total, CHAIN_DP, scatter_dimension=0, tiled=True),
-        lax.psum_scatter(gain_total, CHAIN_DP, scatter_dimension=0, tiled=True),
-        lax.psum_scatter(gate_grad, CHAIN_DP, scatter_dimension=0, tiled=True),
-        lax.psum_scatter(start_total, CHAIN_DP, scatter_dimension=1, tiled=True),
-    )
+    rest = jnp.concatenate(
+        [start_total.T, gain_total[:, None], gate_grad[:, None], jnp.zeros((1024, 126))], axis=1
+    )
+    summed = sum_over_devices(query_total, out_total, key_total, value_total, rest)
+    grad_query, grad_out = summed[:, :1024], summed[:, 1024:2048]
+    grad_key, grad_value = summed[:, 2048:2304], summed[:, 2304:2560]
+    grad_memory = summed[:, 2560:2688].T
+    grad_gain, grad_gate = summed[:, 2688], summed[:, 2689]
     layer_output = result.astype(jnp.bfloat16)[None, None]
     return (
         layer_output,
@@ -259,35 +568,21 @@
 
 
 def solution(mesh):
-    split = Mesh(
-        mesh.devices.reshape(4, 4, 2, mesh.shape["dp"]), ("chain_0", "chain_1", "chain_2", "dp")
-    )
-    placed = (
-        P("dp", CHAIN, None, None),
-        P("dp", CHAIN),
-        P(),
-        P(),
-        P(),
-        P(),
-        P(),
-        P(),
-        P(),
-        P(),
-        P("dp", CHAIN, None, None),
-    )
+    split = Mesh(mesh.devices.reshape(4, 4, 2, 2, 4), AXES)
+    rows = P(("zh", "y"), ("zl", "x", "c"), None, None)
     return jax.shard_map(
         per_device,
         mesh=split,
-        in_specs=placed,
+        in_specs=(rows, P(("zh", "y"), ("zl", "x", "c"))) + (P(),) * 8 + (rows,),
         out_specs=(
-            P("dp", CHAIN, None, None),
-            P(CHAIN_DP, None),
-            P(CHAIN_DP, None),
-            P(CHAIN_DP, None),
-            P(CHAIN_DP, None),
-            P(CHAIN_DP),
-            P(CHAIN_DP),
-            P(None, CHAIN_DP),
+            rows,
+            P(AXES, None),
+            P(AXES, None),
+            P(AXES, None),
+            P(AXES, None),
+            P(AXES),
+            P(AXES),
+            P(None, AXES),
         ),
         check_vma=False,
     )

time: 578 us -> 216 us (0.37)
  waiting for transfers between devices: 345 us -> 0 us
  Pallas kernels: 0 us -> 113 us
  blocking collectives: 107 us -> 0 us
  between operations: 16.3 us -> 2.49 us
  other arithmetic: 30.1 us -> 18.3 us
    unnamed x8 -> x0, waiting for transfers between devices: 199 us -> none
    all_gather x6 -> x0, waiting for transfers between devices: 146 us -> none  [entering(): pieces = jax.tree.map(lambda part: lax.all_gather(part, axis), subtotal)]
    pallas_call x0 -> x3, Pallas kernels: none -> 113 us  [the longest x1 59.7 us: sum_over_devices(): pl.pallas_call(sum_kernel, out_shape=jax.ShapeDtypeStruct((8, TOTAL // 2)...]
    unnamed x1 -> x0, blocking collectives: 78.2 us -> none
    all_gather x4 -> x0, blocking collectives: 28.6 us -> none  [entering(): pieces = jax.tree.map(lambda part: lax.all_gather(part, axis), subtotal)]
    add x5 -> x0, other arithmetic: 10.4 us -> none  [the longest x4 9.35 us: compose(): keep_later[:, None] * add_early + add_later]
    unnamed x228 -> x170, local copies, waits for them, and re-layouts: 16.3 us -> 7.08 us
  transfers between devices with their start and end apart: 7 -> 0, of which waited for: 7 -> 0; matrix products, arithmetic and copies ran while one was open for 5% -> 0% of each run, Pallas kernels for 0% -> 0%
where the time goes in v1:
time: 216 us; the launch traced here: 215 us
  Pallas kernels  113 us (52%)
  matrix products  50.5 us (23%)
  local copies, waits for them, and re-layouts  30.6 us (14%)
  other arithmetic  18.3 us (8%)
  between operations  2.49 us (1%)
    pallas_call x1, Pallas kernels, sum_over_devices(): pl.pallas_call(sum_kernel, out_shape=jax.ShapeDtypeStruct((8, TOTAL // 2)...  59.7 us
    pallas_call x2, Pallas kernels, entering(): pl.pallas_call(functools.partial(scan_kernel, reverse), out_shape=jax.Sha...  53.1 us
    dot_general x3, matrix products, write_part(): written = jnp.dot(context, out_weight, preferred_element_type=jnp.float32)  8.13 us
    dot_general x6, matrix products, attend(): jnp.einsum('gsrk,kgh->rgsh', weights, valued, preferred_element_type=jnp....  7.58 us
    dot_general x6, matrix products, attend(): jnp.einsum('rgsh,kgh->gsrk', grouped, keyed, preferred_element_type=jnp.f...  7.18 us
    unnamed x170, local copies, waits for them, and re-layouts  7.08 us
    dot_general x3, matrix products, read_part(): jnp.dot(context, out_weight, preferred_element_type=jnp.float32)  6.79 us
    dot_general x3, matrix products, prepare(): jnp.dot(normed_rows, query_weight, preferred_element_type=jnp.float32)  5.82 us

profile of v1, /device:TPU:32, one launch (start us, length us, event | category | flops | bytes accessed | tf_op | source)
XLA Modules:
  0.0 214.7 jit_solution(14384876362644558232)
XLA Ops:
  0.6 1.2 fusion.65
  1.9 1.4 convolution_convert_fusion.20
  3.4 1.1 fusion.75
  4.6 1.4 fusion.17
  8.1 1.3 bitcast_reduce_fusion
  9.6 1.0 divide_convert_fusion.1
  11.6 1.0 copy.39
  12.6 1.3 convolution_convert_fusion.16
  14.6 2.1 fusion.107
  19.1 27.9 %prefix.1 = f32[128,1152]{1,0:T(8,128)} custom-call(f32[128,1024]{1,0:T(8,128)} %broadcast_multiply_fusion.add_ref, f32[128,128]{1,0:T(8,128)} %broadcast_in_dim.48.keep_ref), custom_call_target="tpu_custom_call" | custom-call | tf_op jit(solution)/shard_map/prefix/pallas_call | solution.py:326
  47.1 1.0 slice_reduce_fusion
  48.1 1.3 multiply_reduce_fusion.3
  51.9 1.7 copy.44
  53.6 2.1 fusion.18
  55.8 1.8 copy.45
  59.0 1.6 fusion.6
  60.6 1.3 copy-done.8
  63.3 1.7 copy.43
  64.9 3.3 %convolution_convert_fusion.14 = bf16[128,1024]{1,0:T(8,128)(2,1)} fusion(bf16[1024,1024]{1,0:T(8,128)(2,1)} %param.16, bf16[1,1,128,1024]{3,2,1,0:T(8,128)(2,1)} %param.21, f32[128]{0:T(128)S(1)} %copy-done.77), kind=kOutput, calls=%fused_computation.44 | convolution fusion | flops 268828672 | bytes 2621952 | tf_op jit(solution)/shard_map/transpose(jvp())/dot_general | solution.py:416
  68.2 1.8 copy.47
  70.0 2.8 %fusion.5 = (f32[4,4,128]{2,1,0:T(4,128)S(1)}, bf16[4,4,128,256]{2,3,1,0:T(8,128)(2,1)S(1)}, bf16[4,4,128,256]{2,3,1,0:T(8,128)(2,1)S(1)}) fusion(f32[4,256,128,4]{2,1,3,0:T(8,128)} %copy-done.8, f32[4,4,128]{2,1,0:T(4,128)S(1)} %multiply_divide_fusion.1, f32[4,4,128]{2,1,0:T(4,128)S(1)} %get-tuple-element.28, pred[128,256]{0,1:T(8,128)(4,1)S(1)} %get-tuple-element.23, ...), kind=kOutput, calls=%fused_computation.9 | convolution fusion | flops 71825408 | bytes 4653056 | tf_op jit(solution)/shard_map/transpose(jvp(gsrk,kgh->rgsh))/dot_general | solution.py:386
  75.1 1.0 multiply_reduce_fusion
  77.1 25.2 %suffix.1 = f32[128,1152]{1,0:T(8,128)} custom-call(f32[128,1024]{1,0:T(8,128)} %add_add_fusion.1.add_ref, f32[128,128]{1,0:T(8,128)} %broadcast_in_dim.48.keep_ref), custom_call_target="tpu_custom_call" | custom-call | tf_op jit(solution)/shard_map/suffix/pallas_call | solution.py:326
  102.3 1.5 multiply_reduce_fusion.1
  105.0 3.3 %convolution_convert_fusion.11 = bf16[128,1024]{1,0:T(8,128)(2,1)} fusion(bf16[1024,1024]{1,0:T(8,128)(2,1)} %param.16, f32[128,1152]{1,0:T(8,128)} %suffix.1, f32[1024]{0:T(1024)S(1)} %copy-done.50, f32[128]{0:T(128)S(1)} %multiply_multiply_fusion.1, f32[128]{0:T(128)} %copy-done.61), kind=kOutput, calls=%fused_computation.41 | convolution fusion | flops 268959744 | bytes 2888704 | tf_op jit(solution)/shard_map/transpose(jvp())/dot_general | solution.py:441
  108.3 1.8 copy.50
  110.8 1.4 fusion.54
  112.2 1.0 fusion.52
  115.0 1.5 fusion.77
  116.5 1.0 fusion.74
  117.5 2.2 %copy.52 = f32[1024,128]{1,0:T(8,128)} copy(f32[1024,128]{0,1:T(8,128)} %fusion.74) | data formatting | bytes 1048576 | tf_op jit(solution)/shard_map/transpose | solution.py:550
  119.8 1.4 fusion.43
  121.2 1.3 fusion.38
  122.5 1.4 convolution_convert_fusion.7
  123.9 2.0 fusion.16
  128.1 1.9 add.108
  130.0 1.6 fusion.91
  131.7 2.4 %maximum_maximum_fusion.refs_4_ = f32[16,2,32,256]{3,2,1,0:T(8,128)} fusion(f32[16,2,32,1]{3,2,1,0:T(8,128)S(1)} %bitcast.294, f32[16,2,32,1]{3,2,1,0:T(8,128)} %add.108, f32[16,2,32,128]{3,2,1,0:T(8,128)} %bitcast.293, f32[256]{0:T(256)S(1)} %pad.6.clone), kind=kLoop, calls=%fused_computation.95 | loop fusion | flops 786432 | bytes 1582080 | tf_op jit(solution)/shard_map/concatenate | solution.py:549
  134.5 1.4 fusion.9
  136.2 1.4 fusion.12
  138.8 2.8 %convert_add_fusion = f32[1024,1024]{1,0:T(8,128)} fusion(bf16[1024,1024]{1,0:T(8,128)(2,1)S(1)} %fusion.71, bf16[128,1024]{0,1:T(8,128)(2,1)S(1)} %bitcast.288, f32[128,1152]{1,0:T(8,128)S(1)} %copy-done.11, f32[1024]{0:T(1024)S(1)} %copy-done.50, f32[128]{0:T(128)S(1)} %copy-done.75, f32[128]{0:T(128)S(1)} %copy-done.62), kind=kOutput, calls=%fused_computation | convolution fusion | flops 273022976 | bytes 7083008 | tf_op jit(solution)/shard_map/transpose(jvp())/dot_general | solution.py:441
  142.5 2.8 %convert_add_fusion.1 = f32[1024,1024]{1,0:T(8,128)} fusion(bf16[1024,1024]{1,0:T(8,128)(2,1)S(1)} %fusion.87, bf16[128,1024]{0,1:T(8,128)(2,1)S(1)} %bitcast.296, bf16[1,1,128,1024]{3,2,1,0:T(8,128)(2,1)S(1)} %copy-done.7, f32[1024]{0:T(1024)S(1)} %copy-done.42, f32[128]{0:T(128)S(1)} %copy-done.65), kind=kOutput, calls=%fused_computation.1 | convolution fusion | flops 272105472 | bytes 6820352 | tf_op jit(solution)/shard_map/transpose(jvp())/dot_general | solution.py:364
  145.3 59.7 %sum_over_devices.1 = f32[8,1408]{1,0:T(8,128)} custom-call(f32[16,2,32,1024]{3,2,1,0:T(8,128)} %bitcast.280, f32[16,2,32,1024]{3,2,1,0:T(8,128)} %bitcast.279, f32[16,2,32,256]{3,2,1,0:T(8,128)} %bitcast.282, f32[16,2,32,256]{3,2,1,0:T(8,128)} %bitcast.281, f32[16,2,32,256]{3,2,1,0:T(8,128)} %maximum_maximum_fusion.refs_4_), custom_call_target="tpu_custom_call" | custom-call | tf_op jit(solution)/shard_map/sum_over_devices/pallas_call | solution.py:225
  206.5 1.4 slice.49
  207.9 1.3 fusion.106
  209.2 1.3 slice_bitcast_fusion
  210.5 1.5 slice_reduce_fusion.1
  212.0 2.8 %fusion.22 = bf16[1,1,128,1024]{3,2,1,0:T(8,128)(2,1)} fusion(bf16[128,1024]{0,1:T(8,128)(2,1)S(1)} %bitcast.292, bf16[1024,1024]{1,0:T(8,128)(2,1)} %param.16, bf16[1,1,128,1024]{3,2,1,0:T(8,128)(2,1)S(1)} %copy-done.7), kind=kOutput, calls=%fused_computation.53 | convolution fusion | flops 268828672 | bytes 2883584 | tf_op jit(solution)/shard_map/jvp()/dot_general | solution.py:416
  (214 shorter events, 24.1 us)
Async XLA Ops:
  0.6 3.9 %copy-start = (bf16[1024,1024]{1,0:T(8,128)(2,1)S(1)}, bf16[1024,1024]{1,0:T(8,128)(2,1)}, u32[]{:S(2)}) copy-start(bf16[1024,1024]{1,0:T(8,128)(2,1)} %param.13) | copy-start | bytes 6291460
  1.9 8.8 %copy-start.63 = (f32[128]{0:T(128)}, f32[128]{0:T(128)S(1)}, u32[]{:S(2)}) copy-start(f32[128]{0:T(128)S(1)} %add_rsqrt_fusion) | copy-start | bytes 1540
  4.5 3.1 %copy-start.80 = (f32[128]{0:T(128)}, f32[128]{0:T(128)S(1)}, u32[]{:S(2)}) copy-start(f32[128]{0:T(128)S(1)} %fusion.75) | copy-start | bytes 1540
  4.6 4.9 %copy-start.66 = (f32[128]{0:T(128)}, f32[128]{0:T(128)S(1)}, u32[]{:S(2)}) copy-start(f32[128]{0:T(128)S(1)} %fusion.93) | copy-start | bytes 1540
  6.9 3.8 %copy-start.6 = (bf16[1,1,128,1024]{3,2,1,0:T(8,128)(2,1)S(1)}, bf16[1,1,128,1024]{3,2,1,0:T(8,128)(2,1)}, u32[]{:S(2)}) copy-start(bf16[1,1,128,1024]{3,2,1,0:T(8,128)(2,1)} %param.11) | copy-start | bytes 786436
  6.9 3.8 %copy-start.27 = (bf16[1024,256]{1,0:T(8,128)(2,1)S(1)}, bf16[1024,256]{1,0:T(8,128)(2,1)}, u32[]{:S(2)}) copy-start(bf16[1024,256]{1,0:T(8,128)(2,1)} %param.15) | copy-start | bytes 1572868
  6.9 3.8 %copy-start.42 = (f32[1024]{0:T(1024)S(1)}, f32[1024]{0:T(1024)}, u32[]{:S(2)}) copy-start(f32[1024]{0:T(1024)} %param.17) | copy-start | bytes 12292
  11.6 5.1 %copy-start.50 = (f32[1024]{0:T(1024)S(1)}, f32[1024]{0:T(1024)}, u32[]{:S(2)}) copy-start(f32[1024]{0:T(1024)} %param.18) | copy-start | bytes 12292
  12.6 4.7 %copy-start.38 = (bf16[128,256]{0,1:T(8,128)(2,1)}, bf16[128,256]{0,1:T(8,128)(2,1)S(1)}, u32[]{:S(2)}) copy-start(bf16[128,256]{0,1:T(8,128)(2,1)S(1)} %copy.39) | copy-start | bytes 196612
  12.6 4.1 %copy-start.79 = (f32[128]{0:T(128)S(1)}, f32[128]{0:T(128)}, u32[]{:S(2)}) copy-start(f32[128]{0:T(128)} %param.19) | copy-start | bytes 1540
  16.7 31.4 %copy-start.5 = (bf16[128,1024]{1,0:T(8,128)(2,1)S(1)}, bf16[128,1024]{1,0:T(8,128)(2,1)}, u32[]{:S(2)}) copy-start(bf16[128,1024]{1,0:T(8,128)(2,1)} %param.20) | copy-start | bytes 786436
  19.1 32.2 %copy-start.47 = (bf16[128,256]{1,0:T(8,128)(2,1)S(1)}, bf16[128,256]{1,0:T(8,128)(2,1)}, u32[]{:S(2)}) copy-start(bf16[128,256]{1,0:T(8,128)(2,1)} %copy-done.46) | copy-start | bytes 196612
  47.0 4.0 %copy-start.18 = (bf16[1024,256]{1,0:T(8,128)(2,1)S(1)}, bf16[1024,256]{1,0:T(8,128)(2,1)}, u32[]{:S(2)}) copy-start(bf16[1024,256]{1,0:T(8,128)(2,1)} %param.14) | copy-start | bytes 1572868
  58.9 3.4 %copy-start.13 = (bf16[128,1024]{1,0:T(8,128)(2,1)S(1)}, bf16[128,1024]{1,0:T(8,128)(2,1)}, u32[]{:S(2)}) copy-start(bf16[128,1024]{1,0:T(8,128)(2,1)} %copy-done.12) | copy-start | bytes 786436
  59.0 3.4 %copy-start.28 = (bf16[1024,256]{1,0:T(8,128)(2,1)S(1)}, bf16[1024,256]{1,0:T(8,128)(2,1)}, u32[]{:S(2)}) copy-start(bf16[1024,256]{1,0:T(8,128)(2,1)} %param.15) | copy-start | bytes 1572868
  60.5 12.2 %copy-start.51 = (f32[4,4,128]{2,1,0:T(4,128)}, f32[4,4,128]{2,1,0:T(4,128)S(1)}, u32[]{:S(2)}) copy-start(f32[4,4,128]{2,1,0:T(4,128)S(1)} %get-tuple-element.28) | copy-start | bytes 24580
  60.6 2.0 copy-start.45
  60.6 4.4 %copy-start.77 = (f32[128]{0:T(128)S(1)}, f32[128]{0:T(128)}, u32[]{:S(2)}) copy-start(f32[128]{0:T(128)} %get-tuple-element.36) | copy-start | bytes 1540
  62.3 10.5 %copy-start.53 = (f32[4,4,128]{2,1,0:T(4,128)}, f32[4,4,128]{2,1,0:T(4,128)S(1)}, u32[]{:S(2)}) copy-start(f32[4,4,128]{2,1,0:T(4,128)S(1)} %fusion.7) | copy-start | bytes 24580
  70.0 2.8 %copy-start.9 = (f32[4,256,128,4]{2,1,3,0:T(8,128)S(1)}, f32[4,256,128,4]{2,1,3,0:T(8,128)}, u32[]{:S(2)}) copy-start(f32[4,256,128,4]{2,1,3,0:T(8,128)} %copy-done.8) | copy-start | bytes 6291460
  70.0 2.9 %copy-start.33 = (bf16[128,1024]{0,1:T(8,128)(2,1)S(1)}, bf16[128,1024]{0,1:T(8,128)(2,1)}, u32[]{:S(2)}) copy-start(bf16[128,1024]{0,1:T(8,128)(2,1)} %copy.45) | copy-start | bytes 786436
  70.0 2.9 %copy-start.55 = (pred[256,128]{1,0:T(8,128)(4,1)S(1)}, pred[256,128]{1,0:T(8,128)(4,1)}, u32[]{:S(2)}) copy-start(pred[256,128]{1,0:T(8,128)(4,1)} %get-tuple-element.22) | copy-start | bytes 98308
  72.8 1.8 copy-start.21
  72.9 1.8 copy-start.34
  73.7 2.4 %copy-start.49 = (bf16[256,4,64]{0,2,1:T(8,128)(2,1)}, bf16[256,4,64]{0,2,1:T(8,128)(2,1)S(1)}, u32[]{:S(2)}) copy-start(bf16[256,4,64]{0,2,1:T(8,128)(2,1)S(1)} %fusion.32) | copy-start | bytes 393220
  73.8 2.3 %copy-start.36 = (bf16[128,4,64]{0,2,1:T(8,128)(2,1)}, bf16[128,4,64]{0,2,1:T(8,128)(2,1)S(1)}, u32[]{:S(2)}) copy-start(bf16[128,4,64]{0,2,1:T(8,128)(2,1)S(1)} %split.23) | copy-start | bytes 196612
  74.3 1.8 copy-start.83
  110.8 4.2 %copy-start.67 = (f32[128]{0:T(128)S(1)}, f32[128]{0:T(128)}, u32[]{:S(2)}) copy-start(f32[128]{0:T(128)} %copy-done.66) | copy-start | bytes 1540
  114.0 2.4 %copy-start.81 = (f32[128]{0:T(128)S(1)}, f32[128]{0:T(128)}, u32[]{:S(2)}) copy-start(f32[128]{0:T(128)} %copy-done.80) | copy-start | bytes 1540
  114.0 2.4 %copy-start.20 = (f32[128,1024]{1,0:T(8,128)S(1)}, f32[128,1024]{1,0:T(8,128)}, u32[]{:S(2)}) copy-start(f32[128,1024]{1,0:T(8,128)} %add_add_fusion.1.add_ref) | copy-start | bytes 1572868
  114.1 2.5 %copy-start.73 = (f32[128]{0:T(128)S(1)}, f32[128]{0:T(128)}, u32[]{:S(2)}) copy-start(f32[128]{0:T(128)} %copy-done.72) | copy-start | bytes 1540
  116.5 3.3 %copy-start.15 = (bf16[4,4,128,128]{2,3,1,0:T(8,128)(2,1)S(1)}, bf16[4,4,128,128]{2,3,1,0:T(8,128)(2,1)}, u32[]{:S(2)}) copy-start(bf16[4,4,128,128]{2,3,1,0:T(8,128)(2,1)} %divide_convert_fusion.1) | copy-start | bytes 1572868
  116.5 4.7 %copy-start.17 = (bf16[4,128,128,4]{2,1,3,0:T(8,128)(2,1)S(1)}, bf16[4,128,128,4]{2,1,3,0:T(8,128)(2,1)}, u32[]{:S(2)}) copy-start(bf16[4,128,128,4]{2,1,3,0:T(8,128)(2,1)} %copy-done.16) | copy-start | bytes 1572868
  117.5 6.3 %copy-start.52 = (f32[4,4,128]{2,1,0:T(4,128)S(1)}, f32[4,4,128]{2,1,0:T(4,128)}, u32[]{:S(2)}) copy-start(f32[4,4,128]{2,1,0:T(4,128)} %copy-done.51) | copy-start | bytes 24580
  119.7 4.1 %copy-start.10 = (f32[4,256,128,4]{2,1,3,0:T(8,128)S(1)}, f32[4,256,128,4]{2,1,3,0:T(8,128)}, u32[]{:S(2)}) copy-start(f32[4,256,128,4]{2,1,3,0:T(8,128)} %copy-done.8) | copy-start | bytes 6291460
  119.7 4.1 %copy-start.39 = (bf16[256,256]{0,1:T(8,128)(2,1)S(1)}, bf16[256,256]{0,1:T(8,128)(2,1)}, u32[]{:S(2)}) copy-start(bf16[256,256]{0,1:T(8,128)(2,1)} %copy.44) | copy-start | bytes 393220
  119.8 4.1 %copy-start.54 = (f32[4,4,128]{2,1,0:T(4,128)S(1)}, f32[4,4,128]{2,1,0:T(4,128)}, u32[]{:S(2)}) copy-start(f32[4,4,128]{2,1,0:T(4,128)} %copy-done.53) | copy-start | bytes 24580
  119.8 4.1 %copy-start.56 = (pred[256,128]{1,0:T(8,128)(4,1)S(1)}, pred[256,128]{1,0:T(8,128)(4,1)}, u32[]{:S(2)}) copy-start(pred[256,128]{1,0:T(8,128)(4,1)} %get-tuple-element.22) | copy-start | bytes 98308
  119.8 4.1 %copy-start.60 = (f32[4,128,4]{1,2,0:T(4,128)S(1)}, f32[4,128,4]{1,2,0:T(4,128)}, u32[]{:S(2)}) copy-start(f32[4,128,4]{1,2,0:T(4,128)} %copy-done.59) | copy-start | bytes 24580
  121.2 5.7 %copy-start.43 = (bf16[128,4,64]{0,2,1:T(8,128)(2,1)}, bf16[128,4,64]{0,2,1:T(8,128)(2,1)S(1)}, u32[]{:S(2)}) copy-start(bf16[128,4,64]{0,2,1:T(8,128)(2,1)S(1)} %fusion.43) | copy-start | bytes 196612
  126.0 4.1 %copy-start.4 = (f32[128,1024]{1,0:T(8,128)S(1)}, f32[128,1024]{1,0:T(8,128)}, u32[]{:S(2)}) copy-start(f32[128,1024]{1,0:T(8,128)} %copy-done.3) | copy-start | bytes 1572868
  128.1 6.0 %copy-start.14 = (bf16[128,1024]{1,0:T(8,128)(2,1)S(1)}, bf16[128,1024]{1,0:T(8,128)(2,1)}, u32[]{:S(2)}) copy-start(bf16[128,1024]{1,0:T(8,128)(2,1)} %copy-done.12) | copy-start | bytes 786436
  131.6 2.9 %copy-start.44 = (bf16[128,4,64]{0,2,1:T(8,128)(2,1)S(1)}, bf16[128,4,64]{0,2,1:T(8,128)(2,1)}, u32[]{:S(2)}) copy-start(bf16[128,4,64]{0,2,1:T(8,128)(2,1)} %copy-done.43) | copy-start | bytes 196612
  131.6 2.9 %copy-start.65 = (f32[128]{0:T(128)S(1)}, f32[128]{0:T(128)}, u32[]{:S(2)}) copy-start(f32[128]{0:T(128)} %copy-done.63) | copy-start | bytes 1540
  135.9 1.7 copy-start.22
  135.9 1.8 copy-start.41
  138.8 2.8 %copy-start.24 = (bf16[4,128,4,64]{1,3,2,0:T(8,128)(2,1)S(1)}, bf16[4,128,4,64]{1,3,2,0:T(8,128)(2,1)}, u32[]{:S(2)}) copy-start(bf16[4,128,4,64]{1,3,2,0:T(8,128)(2,1)} %copy-done.23) | copy-start | bytes 786436
  138.8 2.8 %copy-start.68 = (f32[128]{0:T(128)S(1)}, f32[128]{0:T(128)}, u32[]{:S(2)}) copy-start(f32[128]{0:T(128)} %copy-done.66) | copy-start | bytes 1540
  (37 other events, 43.0 us)

commit v2 on v1

--- a/solution.py
+++ b/solution.py
@@ -345,104 +345,220 @@
             collective_id=1 if reverse else 0, has_side_effects=True
         ),
         name="suffix" if reverse else "prefix",
-    )(added, jnp.broadcast_to(keep[:, None], (128, 128)))
-    return out[:, 1024], out[:, :1024]
+    )(added, keep)
+    return out
 
 
 epsilon = 1e-05
 score_scale = 0.125
-
-
-def normalize(activations, norm_gain):
-    inverse = lax.rsqrt(jnp.mean(activations * activations, axis=-1, keepdims=True) + epsilon)
-    return (activations * inverse * norm_gain).astype(jnp.bfloat16)
-
-
-def prepare(query_weight, key_weight, value_weight, norm_gain, segment):
-    normed_rows = normalize(segment.astype(jnp.float32), norm_gain)
-    queries = (
-        jnp.dot(normed_rows, query_weight, preferred_element_type=jnp.float32) * score_scale
-    ).astype(jnp.bfloat16)
-    key_rows = jnp.dot(normed_rows, key_weight, preferred_element_type=jnp.float32).astype(
-        jnp.bfloat16
-    )
-    value_rows = jnp.dot(normed_rows, value_weight, preferred_element_type=jnp.float32).astype(
-        jnp.bfloat16
-    )
-    return (queries, key_rows, value_rows)
-
-
-def attend(queries, key_rows, value_rows, allowed):
-    count = queries.shape[0]
-    width = key_rows.shape[0]
-    groups = key_rows.shape[1] // HEAD
-    shared = queries.shape[1] // key_rows.shape[1]
-    grouped = queries.reshape(count, groups, shared, HEAD)
-    keyed = key_rows.reshape(width, groups, HEAD)
-    valued = value_rows.reshape(width, groups, HEAD)
-    scores = jnp.einsum("rgsh,kgh->gsrk", grouped, keyed, preferred_element_type=jnp.float32)
-    scores = jnp.where(allowed, scores, -1e30)
-    weights = jax.nn.softmax(scores, axis=-1).astype(jnp.bfloat16)
-    context = jnp.einsum("gsrk,kgh->rgsh", weights, valued, preferred_element_type=jnp.float32)
-    return context.reshape(count, groups * shared * HEAD).astype(jnp.bfloat16)
-
-
-def read_part(
-    queries,
-    seg_keys,
-    seg_values,
-    key_weight,
-    value_weight,
-    out_weight,
-    norm_gain,
-    memory_in,
-    segment,
-    seg_length,
+F32, BF16 = jnp.float32, jnp.bfloat16
+GROUPS, SHARED, SEG = 4, 4, 128
+
+
+def mul(a, b):
+    return lax.dot_general(a, b, (((1,), (0,)), ((), ())), preferred_element_type=F32)
+
+
+def mul_nt(a, b):
+    return lax.dot_general(a, b, (((1,), (1,)), ((), ())), preferred_element_type=F32)
+
+
+def mul_tn(a, b):
+    return lax.dot_general(a, b, (((0,), (0,)), ((), ())), preferred_element_type=F32)
+
+
+def inverse_of(rows):
+    return lax.rsqrt(jnp.mean(rows * rows, axis=-1, keepdims=True) + epsilon)
+
+
+def normalize(rows, gain):
+    return (rows * inverse_of(rows) * gain).astype(BF16)
+
+
+def normalize_back(rows, gain, d_normed):
+    inverse = inverse_of(rows)
+    scaled = d_normed * gain
+    shared = jnp.mean(scaled * rows, axis=-1, keepdims=True)
+    return inverse * scaled - rows * (inverse * inverse * inverse * shared)
+
+
+def stacked(rows, group):
+    start = group * SHARED * HEAD
+    return jnp.concatenate(
+        [rows[:, start + k * HEAD : start + (k + 1) * HEAD] for k in range(SHARED)], axis=0
+    )
+
+
+def side_by_side(rows):
+    return jnp.concatenate([rows[k * SEG : (k + 1) * SEG] for k in range(SHARED)], axis=1)
+
+
+def of_group(rows, group):
+    return rows[:, group * HEAD : (group + 1) * HEAD]
+
+
+def weights_of(queries, keys, allowed):
+    scores = jnp.where(allowed, mul_nt(queries, keys), -1e30)
+    raised = jnp.exp(scores - jnp.max(scores, axis=-1, keepdims=True))
+    return raised / jnp.sum(raised, axis=-1, keepdims=True)
+
+
+def attend_back(weights, rounded, queries, keys, values, d_context):
+    d_values = mul_tn(rounded, d_context)
+    d_weights = mul_nt(d_context, values).astype(BF16).astype(F32)
+    pulled = jnp.sum(d_weights * weights, axis=-1, keepdims=True)
+    d_scores = (weights * (d_weights - pulled)).astype(BF16)
+    return mul(d_scores, keys).astype(BF16), mul_tn(d_scores, queries), d_values
+
+
+def write_kernel(
+    length_ref, x_ref, wq_ref, wk_ref, wv_ref, wo_ref, gain_ref, vector_ref, bias_ref, start_ref,
+    q_ref, k_ref, v_ref, xn_ref, sn_ref, sq_ref, p_ref, context_ref, written_ref, retain_ref,
+    added_ref,
 ):
-    memory_rows = normalize(memory_in, norm_gain)
-    memory_keys = jnp.dot(memory_rows, key_weight, preferred_element_type=jnp.float32).astype(
-        jnp.bfloat16
-    )
-    memory_values = jnp.dot(memory_rows, value_weight, preferred_element_type=jnp.float32).astype(
-        jnp.bfloat16
-    )
-    key_rows = jnp.concatenate([memory_keys, seg_keys], axis=0)
-    value_rows = jnp.concatenate([memory_values, seg_values], axis=0)
-    count = segment.shape[0]
-    places = jnp.arange(count)
-    causal = (places[None, :] <= places[:, None]) & (places[None, :] < seg_length)
-    allowed = jnp.concatenate([jnp.ones((count, memory_in.shape[0]), dtype=bool), causal], axis=1)
-    context = attend(queries, key_rows, value_rows, allowed)
-    return segment.astype(jnp.float32) + jnp.dot(
-        context, out_weight, preferred_element_type=jnp.float32
-    )
-
-
-def write_part(
-    seg_keys,
-    seg_values,
-    query_weight,
-    out_weight,
-    norm_gain,
-    gate_vector,
-    memory_start,
-    gate_bias,
-    seg_length,
+    length = length_ref[0, 0]
+    gain = gain_ref[...]
+    xn = normalize(x_ref[...].astype(F32), gain)
+    sn = normalize(start_ref[...].astype(F32), gain)
+    xn_ref[...] = xn
+    sn_ref[...] = sn
+    both = (mul(jnp.concatenate([xn, sn], axis=0), wq_ref[...]) * score_scale).astype(BF16)
+    q_ref[...] = both[:SEG]
+    sq = both[SEG:]
+    sq_ref[...] = sq
+    keys = mul(xn, wk_ref[...]).astype(BF16)
+    values = mul(xn, wv_ref[...]).astype(BF16)
+    k_ref[...] = keys
+    v_ref[...] = values
+    allowed = lax.broadcasted_iota(jnp.int32, (SHARED * SEG, SEG), 1) < length
+    contexts = []
+    for group in range(GROUPS):
+        weights = weights_of(stacked(sq, group), of_group(keys, group), allowed).astype(BF16)
+        p_ref[group] = weights
+        contexts.append(side_by_side(mul(weights, of_group(values, group)).astype(BF16)))
+    context = jnp.concatenate(contexts, axis=1)
+    context_ref[...] = context
+    written = mul(context, wo_ref[...])
+    written_ref[...] = written
+    logits = jnp.sum(written * vector_ref[...], axis=-1, keepdims=True) + bias_ref[...]
+    retain = jax.nn.sigmoid(logits)
+    retain_ref[...] = jnp.broadcast_to(retain, (SEG, 128))
+    added_ref[...] = (1.0 - retain) * written
+
+
+def read_kernel(
+    length_ref, x_ref, cot_ref, wk_ref, wv_ref, wo_ref, gain_ref, start_ref, scan_ref,
+    q_ref, k_ref, v_ref,
+    out_ref, memory_ref, mn_ref, context_ref, dr_ref, dq_ref, dk_ref, dv_ref, dmk_ref, dmv_ref,
+    r_ref,
 ):
-    start_rows = normalize(memory_start, norm_gain)
-    slot_queries = (
-        jnp.dot(start_rows, query_weight, preferred_element_type=jnp.float32) * score_scale
-    ).astype(jnp.bfloat16)
-    places = jnp.arange(seg_keys.shape[0])
-    allowed = jnp.broadcast_to(
-        places[None, :] < seg_length, (memory_start.shape[0], seg_keys.shape[0])
-    )
-    context = attend(slot_queries, seg_keys, seg_values, allowed)
-    written = jnp.dot(context, out_weight, preferred_element_type=jnp.float32)
-    retain = jax.nn.sigmoid(
-        gate_bias + jnp.dot(written, gate_vector, precision=lax.Precision.HIGHEST)
-    )
-    return (retain, written)
+    length = length_ref[0, 0]
+    gain = gain_ref[...]
+    memory = scan_ref[:, 1024:1025] * start_ref[...].astype(F32) + scan_ref[:, :1024]
+    memory_ref[...] = memory
+    mn = normalize(memory, gain)
+    mn_ref[...] = mn
+    keys = jnp.concatenate([mul(mn, wk_ref[...]).astype(BF16), k_ref[...]], axis=0)
+    values = jnp.concatenate([mul(mn, wv_ref[...]).astype(BF16), v_ref[...]], axis=0)
+    valid = lax.broadcasted_iota(jnp.int32, (SEG, 1024), 0) < length
+    d_result = jnp.where(valid, cot_ref[...].astype(F32), 0.0).astype(BF16)
+    dr_ref[...] = d_result
+    d_context = mul_nt(d_result, wo_ref[...]).astype(BF16)
+    shape = (SHARED * SEG, 2 * SEG)
+    place = lax.broadcasted_iota(jnp.int32, shape, 1) - SEG
+    row = lax.rem(lax.broadcasted_iota(jnp.int32, shape, 0), SEG)
+    allowed = (place < 0) | ((place <= row) & (place < length))
+    queries = q_ref[...]
+    contexts, d_queries, d_keys, d_values = [], [], [], []
+    for group in range(GROUPS):
+        q, k, v = stacked(queries, group), of_group(keys, group), of_group(values, group)
+        weights = weights_of(q, k, allowed)
+        rounded = weights.astype(BF16)
+        contexts.append(side_by_side(mul(rounded, v).astype(BF16)))
+        dq, dk, dv = attend_back(weights, rounded, q, k, v, stacked(d_context, group))
+        d_queries.append(side_by_side(dq))
+        d_keys.append(dk.astype(BF16))
+        d_values.append(dv.astype(BF16))
+    context = jnp.concatenate(contexts, axis=1)
+    context_ref[...] = context
+    out_ref[...] = (x_ref[...].astype(F32) + mul(context, wo_ref[...])).astype(BF16)
+    dq_ref[...] = jnp.concatenate(d_queries, axis=1)
+    d_key = jnp.concatenate(d_keys, axis=1)
+    d_value = jnp.concatenate(d_values, axis=1)
+    dmk_ref[...] = d_key[:SEG]
+    dmv_ref[...] = d_value[:SEG]
+    dk_ref[...] = d_key[SEG:]
+    dv_ref[...] = d_value[SEG:]
+    d_mn = mul_nt(d_key[:SEG], wk_ref[...]) + mul_nt(d_value[:SEG], wv_ref[...])
+    r_ref[...] = normalize_back(memory, gain, d_mn.astype(BF16).astype(F32))
+
+
+def grads_kernel(
+    later_ref, memory_ref, written_ref, retain_ref, vector_ref, wq_ref, wo_ref, gain_ref,
+    start_ref, scan_ref, r_ref, p_ref, q_ref, sq_ref, k_ref, v_ref, xn_ref, sn_ref, mn_ref,
+    cr_ref, cw_ref, dr_ref, dq_ref, dk_ref, dv_ref, dmk_ref, dmv_ref,
+    gq_ref, go_ref, gk_ref, gv_ref, rest_ref,
+):
+    later = later_ref[:, :1024]
+    written = written_ref[...]
+    retain = retain_ref[:, :1]
+    d_retain = jnp.sum(later * (memory_ref[...] - written), axis=-1, keepdims=True)
+    d_logit = d_retain * retain * (1.0 - retain)
+    gate = jnp.sum(written * d_logit, axis=0, keepdims=True)
+    d_written = ((1.0 - retain) * later + d_logit * vector_ref[...]).astype(BF16)
+    d_context = mul_nt(d_written, wo_ref[...]).astype(BF16)
+    slots, keys, values = sq_ref[...], k_ref[...], v_ref[...]
+    d_slots, d_keys, d_values = [], [], []
+    for group in range(GROUPS):
+        rounded = p_ref[group]
+        dq, dk, dv = attend_back(
+            rounded.astype(F32), rounded, stacked(slots, group), of_group(keys, group),
+            of_group(values, group), stacked(d_context, group),
+        )
+        d_slots.append(side_by_side(dq))
+        d_keys.append(dk.astype(BF16))
+        d_values.append(dv.astype(BF16))
+
+    def added(first, second):
+        return (first.astype(F32) + second.astype(F32)).astype(BF16)
+
+    scale = jnp.asarray(score_scale, BF16)
+    d_slot = jnp.concatenate(d_slots, axis=1) * scale
+    d_key = added(dk_ref[...], jnp.concatenate(d_keys, axis=1))
+    d_value = added(dv_ref[...], jnp.concatenate(d_values, axis=1))
+    left = jnp.concatenate([xn_ref[...], sn_ref[...]], axis=0)
+    right = jnp.concatenate([dq_ref[...] * scale, d_slot], axis=0)
+    normed = jnp.concatenate([xn_ref[...], mn_ref[...]], axis=0)
+    right_key = jnp.concatenate([d_key, dmk_ref[...]], axis=0)
+    right_value = jnp.concatenate([d_value, dmv_ref[...]], axis=0)
+    context = jnp.concatenate([cr_ref[...], cw_ref[...]], axis=0)
+    d_out = jnp.concatenate([dr_ref[...], d_written], axis=0)
+    for block in range(4):
+        rows = slice(block * 256, block * 256 + 256)
+        gq_ref[rows] = mul_tn(left[:, rows], right)
+        go_ref[rows] = mul_tn(context[:, rows], d_out)
+        gk_ref[rows] = mul_tn(normed[:, rows], right_key)
+        gv_ref[rows] = mul_tn(normed[:, rows], right_value)
+    d_sn = mul_nt(d_slot, wq_ref[...]).astype(BF16).astype(F32)
+    start = start_ref[...].astype(F32)
+    total = normalize_back(start, gain_ref[...], d_sn) + scan_ref[:, 1024:1025] * r_ref[...]
+    gates = jnp.broadcast_to(gate, (128, 1024))
+    for block in range(8):
+        rows = slice(block * 128, block * 128 + 128)
+        rest_ref[rows, :128] = jnp.transpose(total[:, rows])
+        rest_ref[rows, 128:] = jnp.transpose(gates[:, rows])
+
+
+def local_kernel(kernel, shapes, operands, name):
+    smem = pl.BlockSpec(memory_space=pltpu.SMEM)
+    return pl.pallas_call(
+        kernel,
+        out_shape=[jax.ShapeDtypeStruct(shape, dtype) for shape, dtype in shapes],
+        in_specs=[smem if a.dtype == jnp.int32 else VMEM_SPEC for a in operands],
+        out_specs=[VMEM_SPEC] * len(shapes),
+        compiler_params=pltpu.CompilerParams(vmem_limit_bytes=60 << 20),
+        name=name,
+    )(*operands)
 
 
 def per_device(
@@ -458,105 +574,51 @@
     memory_init,
     cotangent,
 ):
-    segment = segments[0, 0]
-    seg_length = lengths[0, 0]
-    memory_start = memory_init.astype(jnp.float32)
-
-    def prepared(query_part, key_part, value_part, gain_part):
-        return prepare(query_part, key_part, value_part, gain_part, segment)
-
-    (queries, seg_keys, seg_values), prep_back = jax.vjp(
-        prepared, query_weight, key_weight, value_weight, norm_gain
-    )
-
-    def writing(keys_in, values_in, query_part, out_part, gain_part, vector_part, start_part):
-        return write_part(
-            keys_in,
-            values_in,
-            query_part,
-            out_part,
-            gain_part,
-            vector_part,
-            start_part,
-            gate_bias,
-            seg_length,
-        )
-
-    (retain, written), write_back = jax.vjp(
-        writing,
-        seg_keys,
-        seg_values,
-        query_weight,
-        out_weight,
-        norm_gain,
-        gate_vector,
-        memory_start,
-    )
-    prefix_keep, prefix_add = entering(retain, (1.0 - retain)[:, None] * written, False)
-    memory_in = prefix_keep[:, None] * memory_start + prefix_add
-
-    def reading(
-        queries_in, keys_in, values_in, key_part, value_part, out_part, gain_part, memory_part
-    ):
-        return read_part(
-            queries_in,
-            keys_in,
-            values_in,
-            key_part,
-            value_part,
-            out_part,
-            gain_part,
-            memory_part,
-            segment,
-            seg_length,
-        )
-
-    result, read_back = jax.vjp(
-        reading,
-        queries,
-        seg_keys,
-        seg_values,
-        key_weight,
-        value_weight,
-        out_weight,
-        norm_gain,
-        memory_in,
-    )
-    valid_rows = (jnp.arange(segment.shape[0]) < seg_length)[:, None]
-    d_result = cotangent[0, 0].astype(jnp.float32) * valid_rows
-    d_queries, d_keys_read, d_values_read, key_read, value_read, out_read, gain_read, d_memory = (
-        read_back(d_result)
-    )
-    later_keep, later_grad = entering(retain, d_memory, True)
-    d_retain = jnp.sum(later_grad * (memory_in - written), axis=1)
-    d_written = (1.0 - retain)[:, None] * later_grad
-    d_keys_write, d_values_write, query_write, out_write, gain_write, gate_grad, start_grad = (
-        write_back((d_retain, d_written))
-    )
-    d_keys = (d_keys_read.astype(jnp.float32) + d_keys_write.astype(jnp.float32)).astype(
-        jnp.bfloat16
-    )
-    d_values = (d_values_read.astype(jnp.float32) + d_values_write.astype(jnp.float32)).astype(
-        jnp.bfloat16
-    )
-    query_prep, key_prep, value_prep, gain_prep = prep_back((d_queries, d_keys, d_values))
-    query_total = query_write.astype(jnp.float32) + query_prep.astype(jnp.float32)
-    gain_total = gain_read + gain_write + gain_prep
-    start_total = start_grad + prefix_keep[:, None] * d_memory
-    key_total = key_read.astype(jnp.float32) + key_prep.astype(jnp.float32)
-    value_total = value_read.astype(jnp.float32) + value_prep.astype(jnp.float32)
-    out_total = out_read.astype(jnp.float32) + out_write.astype(jnp.float32)
-    rest = jnp.concatenate(
-        [start_total.T, gain_total[:, None], gate_grad[:, None], jnp.zeros((1024, 126))], axis=1
-    )
-    summed = sum_over_devices(query_total, out_total, key_total, value_total, rest)
+    segment, cot = segments[0, 0], cotangent[0, 0]
+    gain, vector, bias = norm_gain[None], gate_vector[None], gate_bias[:, None]
+    wide, narrow = ((SEG, 1024), BF16), ((SEG, 256), BF16)
+    full = ((SEG, 1024), F32)
+    q, k, v, xn, sn, sq, p, cw, written, retain, added = local_kernel(
+        write_kernel,
+        [wide, narrow, narrow, wide, wide, wide, ((GROUPS, SHARED * SEG, SEG), BF16), wide, full,
+         ((SEG, 128), F32), full],
+        (lengths, segment, query_weight, key_weight, value_weight, out_weight, gain, vector, bias,
+         memory_init),
+        "write_forward",
+    )
+    scan = entering(retain, added, False)
+    output, memory, mn, cr, dr, dq, dk, dv, dmk, dmv, r = local_kernel(
+        read_kernel,
+        [wide, full, wide, wide, wide, wide, narrow, narrow, narrow, narrow, full],
+        (lengths, segment, cot, key_weight, value_weight, out_weight, gain, memory_init, scan, q,
+         k, v),
+        "read_both",
+    )
+    later = entering(retain, r, True)
+    sums = local_kernel(
+        grads_kernel,
+        [((1024, n), F32) for n in (1024, 1024, 256, 256, 256)],
+        (later, memory, written, retain, vector, query_weight, out_weight, gain, memory_init, scan,
+         r, p, q, sq, k, v, xn, sn, mn, cr, cw, dr, dq, dk, dv, dmk, dmv),
+        "gradients",
+    )
+    summed = sum_over_devices(*sums)
     grad_query, grad_out = summed[:, :1024], summed[:, 1024:2048]
     grad_key, grad_value = summed[:, 2048:2304], summed[:, 2304:2560]
     grad_memory = summed[:, 2560:2688].T
-    grad_gain, grad_gate = summed[:, 2688], summed[:, 2689]
-    layer_output = result.astype(jnp.bfloat16)[None, None]
+    grad_gate = summed[:, 2688]
+    place = lax.axis_index(AXES)
+
+    def mine(array):
+        return lax.dynamic_slice_in_dim(array, place * 4, 4, 0).astype(F32)
+
+    grad_gain = (
+        jnp.sum(mine(query_weight) * grad_query, axis=1)
+        + jnp.sum(mine(key_weight) * grad_key, axis=1)
+        + jnp.sum(mine(value_weight) * grad_value, axis=1)
+    ) / mine(norm_gain)
     return (
-        layer_output,
+        output[None, None],
         grad_query,
         grad_key,
         grad_value,

time: 216 us -> 151 us (0.70)
  matrix products: 50.5 us -> 0 us
  Pallas kernels: 113 us -> 140 us
  local copies, waits for them, and re-layouts: 30.6 us -> 4.83 us
  other arithmetic: 18.3 us -> 4.27 us
    dot_general x38 -> x0, matrix products: 50.5 us -> none  [the longest x3 8.13 us: write_part(): written = jnp.dot(context, out_weight, preferred_element_type=jnp.float32)]
    pallas_call x0 -> x3, Pallas kernels: none -> 26.8 us  [local_kernel(): pl.pallas_call(kernel, out_shape=[jax.ShapeDtypeStruct(shape, dtype) for...]
    convert_element_type x6 -> x0, local copies, waits for them, and re-layouts: 7.32 us -> none  [the longest x1 1.81 us: prepare(): queries = (jnp.dot(normed_rows, query_weight, preferred_element_type=jnp....]
    unnamed x170 -> x0, local copies, waits for them, and re-layouts: 7.08 us -> none
    concatenate x4 -> x0, other arithmetic: 4.38 us -> none  [the longest x1 2.42 us: per_device(): jnp.concatenate([start_total.T, gain_total[:, None], gate_grad[:, None],...]
    slice x4 -> x1, local copies, waits for them, and re-layouts: 5.15 us -> 1.31 us  [per_device(): grad_gate = summed[:, 2688]]
    concatenate x3 -> x0, local copies, waits for them, and re-layouts: 3.41 us -> none  [the longest x1 1.68 us: read_part(): key_rows = jnp.concatenate([memory_keys, seg_keys], axis=0)]
    reduce_sum x6 -> x2, other arithmetic: 5.67 us -> 2.98 us  [the longest x1 1.51 us: per_device(): jnp.sum(mine(query_weight) * grad_query, axis=1)]
where the time goes in v2:
time: 151 us; the launch traced here: 150 us
  Pallas kernels  140 us (93%)
  local copies, waits for them, and re-layouts  4.83 us (3%)
  other arithmetic  4.27 us (3%)
    pallas_call x1, Pallas kernels, sum_over_devices(): pl.pallas_call(sum_kernel, out_shape=jax.ShapeDtypeStruct((8, TOTAL // 2)...  59.8 us
    pallas_call x2, Pallas kernels, entering(): pl.pallas_call(functools.partial(scan_kernel, reverse), out_shape=jax.Sha...  53.1 us
    pallas_call x3, Pallas kernels, local_kernel(): pl.pallas_call(kernel, out_shape=[jax.ShapeDtypeStruct(shape, dtype) for...  26.8 us

profile of v2, /device:TPU:32, one launch (start us, length us, event | category | flops | bytes accessed | tf_op | source)
XLA Modules:
  0.0 150.2 jit_solution(1366538400619527768)
XLA Ops:
  1.3 1.4 copy.20.bias_ref
  2.7 6.0 %write_forward.1 = (bf16[128,1024]{1,0:T(8,128)(2,1)}, bf16[128,256]{1,0:T(8,128)(2,1)}, bf16[128,256]{1,0:T(8,128)(2,1)}, bf16[128,1024]{1,0:T(8,128)(2,1)}, bf...) custom-call(s32[1,1]{1,0:T(1,128)S(6)} %copy.21.length_ref, ...), custom_call_target="tpu_custom_call" | custom-call | tf_op jit(solution)/shard_map/write_forward/pallas_call | solution.py:554
  8.7 27.9 %prefix.1.scan_ref = f32[128,1152]{1,0:T(8,128)} custom-call(f32[128,1024]{1,0:T(8,128)} %get-tuple-element.35.add_ref, f32[128,128]{1,0:T(8,128)} %get-tuple-element.36.keep_ref.retain_ref), custom_call_target="tpu_custom_call" | custom-call | tf_op jit(solution)/shard_map/prefix/pallas_call | solution.py:326
  36.6 8.7 %read_both.1 = (bf16[128,1024]{1,0:T(8,128)(2,1)}, f32[128,1024]{1,0:T(8,128)}, bf16[128,1024]{1,0:T(8,128)(2,1)}, bf16[128,1024]{1,0:T(8,128)(2,1)}, bf16[128,1...) custom-call(s32[1,1]{1,0:T(1,128)S(6)} %copy.21.length_ref, ...), custom_call_target="tpu_custom_call" | custom-call | tf_op jit(solution)/shard_map/read_both/pallas_call | solution.py:554
  45.3 25.3 %suffix.1.later_ref = f32[128,1152]{1,0:T(8,128)} custom-call(f32[128,1024]{1,0:T(8,128)} %get-tuple-element.41.add_ref.r_ref, f32[128,128]{1,0:T(8,128)} %get-tuple-element.36.keep_ref.retain_ref), custom_call_target="tpu_custom_call" | custom-call | tf_op jit(solution)/shard_map/suffix/pallas_call | solution.py:326
  70.5 12.1 %gradients.1 = (f32[1024,1024]{1,0:T(8,128)}, f32[1024,1024]{1,0:T(8,128)}, f32[1024,256]{1,0:T(8,128)}, f32[1024,256]{1,0:T(8,128)}, f32[1024,256]{1,0:T(8,128)}) custom-call(f32[128,1152]{1,0:T(8,128)} %suffix.1.later_ref, f32[128,1024]{1,0:T(8,128)} %get-tuple-element.42.memory_ref, f32[128,1024]{1,0:T(8,128)} %get-tuple-element.43.written_ref, ...), custom_call_target="tpu_custom_call" | custom-call | tf_op jit(solution)/shard_map/gradients/pallas_call | solution.py:554
  82.6 59.8 %sum_over_devices.1 = f32[8,1408]{1,0:T(8,128)} custom-call(f32[16,2,32,1024]{3,2,1,0:T(8,128)} %bitcast.13, f32[16,2,32,1024]{3,2,1,0:T(8,128)} %bitcast.14, f32[16,2,32,256]{3,2,1,0:T(8,128)} %bitcast.15, f32[16,2,32,256]{3,2,1,0:T(8,128)} %bitcast.16, f32[16,2,32,256]{3,2,1,0:T(8,128)} %bitcast.17), custom_call_target="tpu_custom_call" | custom-call | tf_op jit(solution)/shard_map/sum_over_devices/pallas_call | solution.py:225
  142.4 0.9 fusion
  143.3 1.5 %multiply_reduce_fusion = (f32[4]{0:T(128)S(1)}, f32[4,1024]{1,0:T(4,128)}, f32[4,1024]{1,0:T(4,128)}) fusion(bf16[1024,1024]{1,0:T(8,128)(2,1)} %wq_ref.3, s32[]{:T(128)S(6)} %select_n.2, f32[8,1408]{1,0:T(8,128)} %sum_over_devices.1, f32[4,1408]{1,0:T(4,128)S(1)} %get-tuple-element.69, f32[4,1408]{1,0:T(4,128)S(1)} %get-tuple-element.68), kind=kLoop, calls=%fused_computation.1 | loop fusion | flops 16380 | bytes 102420 | tf_op jit(solution)/shard_map/reduce_sum | solution.py:616
  144.8 1.5 multiply_reduce_fusion.1
  146.3 1.3 dynamic-slice_divide_fusion
  147.6 1.3 slice_bitcast_fusion
  148.9 1.3 slice_reduce_fusion

commit v3 on v2

--- a/solution.py
+++ b/solution.py
@@ -9,6 +9,7 @@
 from jax.sharding import PartitionSpec as P
 
 HEAD = 64
+F32, BF16 = jnp.float32, jnp.bfloat16
 AXES = ("zl", "x", "c", "zh", "y")
 MESH = pl.DeviceIdType.MESH
 VMEM_SPEC = pl.BlockSpec(memory_space=pltpu.VMEM)
@@ -94,78 +95,102 @@
 
 
 ORDERS = (("x", "y", "z"), ("y", "z", "x"), ("z", "x", "y"))
-WIDTHS = ((1024,), (1024,), (256, 256, 256))
+WIDTHS = ((1024,), (1024,), (512, 256))
 TOTAL = 2816
 
 
 def sum_kernel(*refs):
-    inputs, refs = refs[:5], refs[5:]
-    out_ref, refs = refs[0], refs[1:]
-    landed, refs = refs[:5], refs[5:]
+    left, right, context, d_out, normed, pair, rest, gain, wq, wk, wv = refs[:11]
+    out_ref, refs = refs[11], refs[12:]
+    products, refs = refs[:3], refs[3:]
+    landed, refs = refs[:4], refs[4:]
     works, refs = refs[:3], refs[3:]
     rings_of, refs = refs[:18], refs[18:]
-    sent, mate, fold_in, core_send, core_receive, ring_send, ring_receive, fold_sems = refs
+    rows_of, refs = refs[:3], refs[3:]
+    sent, mate, fold_in, core_send, core_receive, ring_send, ring_receive, fold_sems, row_sems = refs
     core = lax.axis_index("c")
     other = {"c": 1 - core}
     far = z_shift(4)
-    greet(
-        [other, far]
-        + [shift(axis, step) for axis in ("x", "y", "z") for step in (1, -1)]
-    )
+    place = lax.axis_index(AXES)
+    base = pl.ds(pl.multiple_of(lax.div(place, 4) * 16, 16), 16)
+    row_copies = [
+        pltpu.make_async_copy(w.at[base], rows, row_sems.at[k])
+        for k, (w, rows) in enumerate(zip((wq, wk, wv), rows_of))
+    ]
+    for copy in row_copies:
+        copy.start()
+    peers = [other, far] + [shift(axis, step) for axis in ("x", "y", "z") for step in (1, -1)]
+    barrier = pltpu.get_barrier_semaphore()
+    for device in peers:
+        pl.semaphore_signal(barrier, inc=1, device_id=device, device_id_type=MESH)
     core_copies = []
-    for k in range(5):
-        copy = remote(
-            inputs[k].at[:, 1 - core], landed[k], core_send.at[k], core_receive.at[k], other
-        )
+
+    def push_core(source, target):
+        n = len(core_copies)
+        copy = remote(source, target, core_send.at[n], core_receive.at[n], other)
         copy.start()
         core_copies.append(copy)
-    rings = []
-    k = 0
-    for part in range(3):
-        order = ORDERS[part]
-        work = works[part]
+
+    def product(member, block, factor, other_factor):
+        value = mul_tn(factor[:, block * 256 : block * 256 + 256], other_factor[...])
+        products[member][block * 4 : block * 4 + 4] = value.reshape(4, 2, 32, value.shape[1])
+
+    def product_and_push(member, factor, other_factor):
+        for block in range(4):
+            product(member, block, factor, other_factor)
+            if member == 0 and block == 0:
+                pl.semaphore_wait(barrier, len(peers))
+                push_core(rest.at[:, 1 - core], landed[3])
+            blocks = pl.ds(block * 4, 4)
+            push_core(products[member].at[blocks, 1 - core], landed[member].at[blocks])
+
+    members = [((0, 0),), ((1, 0),), ((2, 0), (3, 512))]
+    sources = tuple(products) + (rest,)
+
+    def build_part(part):
+        order, work = ORDERS[part], works[part]
         half_width = sum(WIDTHS[part]) // 2
-        members = []
-        start = 0
-        for width in WIDTHS[part]:
-            members.append((k, width, start))
-            core_copies[k].wait_recv()
-            k += 1
-            start += width
-
-        def build(zl, carry, members=members, order=order, work=work, half_width=half_width):
+
+        def build(zl, carry):
             for x in range(4):
                 block = zl * 4 + x
-                for member, width, start in members:
-                    for col in range(0, width, 128):
+                for member, start in members[part]:
+                    for col in range(0, sources[member].shape[3], 128):
                         cols = pl.ds(col, 128)
                         half = (start + col) // half_width
                         to = pl.ds((start + col) % half_width, 128)
                         rows = (
-                            inputs[member][block, core, :, cols] + landed[member][block, :, cols]
+                            sources[member][block, core, :, cols] + landed[member][block, :, cols]
                         )
                         low = lax.broadcasted_iota(jnp.int32, (8, 128), 0) < 4
-                        for pair in range(2):
-                            a = rows[pair * 8 : pair * 8 + 8]
-                            b = rows[16 + pair * 8 : 24 + pair * 8]
+                        for pair_at in range(2):
+                            a = rows[pair_at * 8 : pair_at * 8 + 8]
+                            b = rows[16 + pair_at * 8 : 24 + pair_at * 8]
                             tiles = (
                                 jnp.where(low, a, pltpu.roll(b, 4, 0)),
                                 jnp.where(low, pltpu.roll(a, 4, 0), b),
                             )
                             for bit in range(2):
-                                where = {"z": zl, "x": x, "y": pair * 2 + bit}
+                                where = {"z": zl, "x": x, "y": pair_at * 2 + bit}
                                 index = (half,) + tuple(where[axis] for axis in order)
                                 work[index + (slice(None), to)] = tiles[bit]
             return carry
 
         lax.fori_loop(0, 4, build, 0)
+
+    rings = []
+
+    def begin(part, waited):
+        for n in waited:
+            core_copies[n].wait_recv()
+        build_part(part)
         stages = []
         for stage in range(3):
             n = part * 3 + stage
             stages.append(
                 Ring(
-                    order[stage],
-                    work if stage == 0 else rings_of[2 * (n - 1) + 1],
+                    ORDERS[part][stage],
+                    works[part] if stage == 0 else rings_of[2 * (n - 1) + 1],
                     rings_of[2 * n],
                     rings_of[2 * n + 1],
                     ring_send.at[n],
@@ -174,6 +199,13 @@
             )
         rings.append(stages)
         stages[0].first()
+
+    product_and_push(0, left, right)
+    product_and_push(1, context, d_out)
+    begin(0, (1, 2, 3, 4))
+    product_and_push(2, normed, pair)
+    begin(1, (5, 6, 7, 8))
+    begin(2, (0, 9, 10, 11, 12))
     for stage in range(3):
         for part in range(3):
             rings[part][stage].second()
@@ -201,39 +233,74 @@
     for stages in rings:
         for ring in stages:
             ring.drain()
+    for copy in row_copies:
+        copy.wait()
+    part_of_16 = lax.rem(place, 4)
+    weights = []
+    for rows in rows_of:
+        loaded = rows[...].astype(F32)
+        tile = jnp.where(part_of_16 >= 2, loaded[8:], loaded[:8])
+        weights.append(jnp.where(lax.rem(place, 2) == 1, pltpu.roll(tile, 4, 0), tile))
+    spot = place * 4 + lax.broadcasted_iota(jnp.int32, (8, 1024), 0)
+    here = lax.broadcasted_iota(jnp.int32, (8, 1024), 1) == spot
+    low = lax.broadcasted_iota(jnp.int32, (8, 1), 0) < 4
+    gains = jnp.sum(jnp.where(here, gain[...], 0.0), axis=1, keepdims=True)
+    gains = jnp.where(low, gains, 1.0)
     last.wait()
-    out_ref[...] = mate[...] + fold_in[...]
-
-
-def sum_over_devices(*arrays):
-    f32 = jnp.float32
-    scratch = [pltpu.VMEM((16, 32, a.shape[1]), f32) for a in arrays]
-    halves = [sum(widths) // 2 for widths in WIDTHS]
-    scratch += [pltpu.VMEM((2, 4, 4, 4, 8, n), f32) for n in halves]
+    short = mate[...] + fold_in[...]
+    full = jnp.concatenate([short, pltpu.roll(short, 4, 0)], axis=1)
+    of_gain = (
+        jnp.sum(weights[0] * full[:, :1024], axis=1, keepdims=True)
+        + jnp.sum(weights[1] * full[:, 2048:2304], axis=1, keepdims=True)
+        + jnp.sum(weights[2] * full[:, 2304:2560], axis=1, keepdims=True)
+    ) / gains
+    out_ref[:, :TOTAL] = full
+    out_ref[:, TOTAL:] = jnp.broadcast_to(of_gain, (8, 128))
+
+
+def sum_over_devices(left, right, context, d_out, normed, pair, rest, gain, wq, wk, wv):
+    widths = (1024, 1024, 512, 256)
+    scratch = [pltpu.VMEM((16, 2, 32, n), F32) for n in widths[:3]]
+    scratch += [pltpu.VMEM((16, 32, n), F32) for n in widths]
+    halves = [sum(w) // 2 for w in WIDTHS]
+    scratch += [pltpu.VMEM((2, 4, 4, 4, 8, n), F32) for n in halves]
     for n in halves:
         for stage in range(3):
-            rest = (4,) * (2 - stage) + (8, n)
-            scratch += [pltpu.VMEM((6,) + rest, f32), pltpu.VMEM((2,) + rest, f32)]
-    scratch += [pltpu.VMEM((8, TOTAL // 2), f32)] * 3
+            tail = (4,) * (2 - stage) + (8, n)
+            scratch += [pltpu.VMEM((6,) + tail, F32), pltpu.VMEM((2,) + tail, F32)]
+    scratch += [pltpu.VMEM((16, n), BF16) for n in (1024, 256, 256)]
+    scratch += [pltpu.VMEM((8, TOTAL // 2), F32)] * 3
     scratch += [
-        pltpu.SemaphoreType.DMA((5,)),
-        pltpu.SemaphoreType.DMA((5,)),
+        pltpu.SemaphoreType.DMA((13,)),
+        pltpu.SemaphoreType.DMA((13,)),
         pltpu.SemaphoreType.DMA((9, 6)),
         pltpu.SemaphoreType.DMA((9, 6)),
         pltpu.SemaphoreType.DMA((2,)),
+        pltpu.SemaphoreType.DMA((3,)),
     ]
-    out = pl.pallas_call(
+    return pl.pallas_call(
         sum_kernel,
-        out_shape=jax.ShapeDtypeStruct((8, TOTAL // 2), f32),
-        in_specs=[VMEM_SPEC] * 5,
+        out_shape=jax.ShapeDtypeStruct((8, TOTAL + 128), F32),
+        in_specs=[VMEM_SPEC] * 8 + [pl.BlockSpec(memory_space=pl.ANY)] * 3,
         out_specs=VMEM_SPEC,
         scratch_shapes=scratch,
         compiler_params=pltpu.CompilerParams(
             collective_id=2, has_side_effects=True, vmem_limit_bytes=60 << 20
         ),
         name="sum_over_devices",
-    )(*[a.reshape(16, 2, 32, a.shape[1]) for a in arrays])
-    return jnp.concatenate([out[:4], out[4:]], axis=1)
+    )(left, right, context, d_out, normed, pair, rest.reshape(16, 2, 32, 256), gain, wq, wk, wv)
+
+
+def finish_kernel(full, gq, go, gk, gv, gain, gate, memory):
+    gq[...] = full[:4, :1024]
+    go[...] = full[:4, 1024:2048]
+    gk[...] = full[:4, 2048:2304]
+    gv[...] = full[:4, 2304:2560]
+    rows = jnp.concatenate([full[:, 2560:2688]] + [jnp.zeros((120, 128), F32)], axis=0)
+    memory[...] = jnp.transpose(rows)[:, :4]
+    for ref, start in ((gate, 2688), (gain, TOTAL)):
+        rows = jnp.concatenate([full[:, start : start + 128], jnp.zeros((120, 128), F32)], axis=0)
+        ref[...] = jnp.transpose(rows)[:1, :4]
 
 
 WIDE = 1152
@@ -351,7 +418,6 @@
 
 epsilon = 1e-05
 score_scale = 0.125
-F32, BF16 = jnp.float32, jnp.bfloat16
 GROUPS, SHARED, SEG = 4, 4, 128
 
 
@@ -413,16 +479,16 @@
 
 def write_kernel(
     length_ref, x_ref, wq_ref, wk_ref, wv_ref, wo_ref, gain_ref, vector_ref, bias_ref, start_ref,
-    q_ref, k_ref, v_ref, xn_ref, sn_ref, sq_ref, p_ref, context_ref, written_ref, retain_ref,
+    q_ref, k_ref, v_ref, left_ref, sq_ref, p_ref, context_ref, written_ref, retain_ref,
     added_ref,
 ):
     length = length_ref[0, 0]
     gain = gain_ref[...]
     xn = normalize(x_ref[...].astype(F32), gain)
     sn = normalize(start_ref[...].astype(F32), gain)
-    xn_ref[...] = xn
-    sn_ref[...] = sn
-    both = (mul(jnp.concatenate([xn, sn], axis=0), wq_ref[...]) * score_scale).astype(BF16)
+    left = jnp.concatenate([xn, sn], axis=0)
+    left_ref[...] = left
+    both = (mul(left, wq_ref[...]) * score_scale).astype(BF16)
     q_ref[...] = both[:SEG]
     sq = both[SEG:]
     sq_ref[...] = sq
@@ -440,7 +506,8 @@
     context_ref[...] = context
     written = mul(context, wo_ref[...])
     written_ref[...] = written
-    logits = jnp.sum(written * vector_ref[...], axis=-1, keepdims=True) + bias_ref[...]
+    bias = jnp.transpose(jnp.broadcast_to(bias_ref[...], (128, 128)))[:, :1]
+    logits = jnp.sum(written * vector_ref[...], axis=-1, keepdims=True) + bias
     retain = jax.nn.sigmoid(logits)
     retain_ref[...] = jnp.broadcast_to(retain, (SEG, 128))
     added_ref[...] = (1.0 - retain) * written
@@ -493,11 +560,11 @@
     r_ref[...] = normalize_back(memory, gain, d_mn.astype(BF16).astype(F32))
 
 
-def grads_kernel(
+def back_kernel(
     later_ref, memory_ref, written_ref, retain_ref, vector_ref, wq_ref, wo_ref, gain_ref,
-    start_ref, scan_ref, r_ref, p_ref, q_ref, sq_ref, k_ref, v_ref, xn_ref, sn_ref, mn_ref,
+    start_ref, scan_ref, r_ref, p_ref, sq_ref, k_ref, v_ref, left_ref, mn_ref,
     cr_ref, cw_ref, dr_ref, dq_ref, dk_ref, dv_ref, dmk_ref, dmv_ref,
-    gq_ref, go_ref, gk_ref, gv_ref, rest_ref,
+    right_ref, context_ref, dout_ref, normed_ref, pair_ref, rest_ref,
 ):
     later = later_ref[:, :1024]
     written = written_ref[...]
@@ -524,21 +591,18 @@
 
     scale = jnp.asarray(score_scale, BF16)
     d_slot = jnp.concatenate(d_slots, axis=1) * scale
-    d_key = added(dk_ref[...], jnp.concatenate(d_keys, axis=1))
-    d_value = added(dv_ref[...], jnp.concatenate(d_values, axis=1))
-    left = jnp.concatenate([xn_ref[...], sn_ref[...]], axis=0)
-    right = jnp.concatenate([dq_ref[...] * scale, d_slot], axis=0)
-    normed = jnp.concatenate([xn_ref[...], mn_ref[...]], axis=0)
-    right_key = jnp.concatenate([d_key, dmk_ref[...]], axis=0)
-    right_value = jnp.concatenate([d_value, dmv_ref[...]], axis=0)
-    context = jnp.concatenate([cr_ref[...], cw_ref[...]], axis=0)
-    d_out = jnp.concatenate([dr_ref[...], d_written], axis=0)
-    for block in range(4):
-        rows = slice(block * 256, block * 256 + 256)
-        gq_ref[rows] = mul_tn(left[:, rows], right)
-        go_ref[rows] = mul_tn(context[:, rows], d_out)
-        gk_ref[rows] = mul_tn(normed[:, rows], right_key)
-        gv_ref[rows] = mul_tn(normed[:, rows], right_value)
+    right_ref[:SEG] = dq_ref[...] * scale
+    right_ref[SEG:] = d_slot
+    pair_ref[:SEG, :256] = added(dk_ref[...], jnp.concatenate(d_keys, axis=1))
+    pair_ref[:SEG, 256:] = added(dv_ref[...], jnp.concatenate(d_values, axis=1))
+    pair_ref[SEG:, :256] = dmk_ref[...]
+    pair_ref[SEG:, 256:] = dmv_ref[...]
+    normed_ref[:SEG] = left_ref[:SEG]
+    normed_ref[SEG:] = mn_ref[...]
+    context_ref[:SEG] = cr_ref[...]
+    context_ref[SEG:] = cw_ref[...]
+    dout_ref[:SEG] = dr_ref[...]
+    dout_ref[SEG:] = d_written
     d_sn = mul_nt(d_slot, wq_ref[...]).astype(BF16).astype(F32)
     start = start_ref[...].astype(F32)
     total = normalize_back(start, gain_ref[...], d_sn) + scan_ref[:, 1024:1025] * r_ref[...]
@@ -575,12 +639,12 @@
     cotangent,
 ):
     segment, cot = segments[0, 0], cotangent[0, 0]
-    gain, vector, bias = norm_gain[None], gate_vector[None], gate_bias[:, None]
+    gain, vector, bias = norm_gain[None], gate_vector[None], gate_bias[None]
     wide, narrow = ((SEG, 1024), BF16), ((SEG, 256), BF16)
-    full = ((SEG, 1024), F32)
-    q, k, v, xn, sn, sq, p, cw, written, retain, added = local_kernel(
+    full, double = ((SEG, 1024), F32), ((2 * SEG, 1024), BF16)
+    q, k, v, left, sq, p, cw, written, retain, added = local_kernel(
         write_kernel,
-        [wide, narrow, narrow, wide, wide, wide, ((GROUPS, SHARED * SEG, SEG), BF16), wide, full,
+        [wide, narrow, narrow, double, wide, ((GROUPS, SHARED * SEG, SEG), BF16), wide, full,
          ((SEG, 128), F32), full],
         (lengths, segment, query_weight, key_weight, value_weight, out_weight, gain, vector, bias,
          memory_init),
@@ -595,28 +659,25 @@
         "read_both",
     )
     later = entering(retain, r, True)
-    sums = local_kernel(
-        grads_kernel,
-        [((1024, n), F32) for n in (1024, 1024, 256, 256, 256)],
+    right, context, d_out, normed, pair, rest = local_kernel(
+        back_kernel,
+        [double, double, double, double, ((2 * SEG, 512), BF16), ((1024, 256), F32)],
         (later, memory, written, retain, vector, query_weight, out_weight, gain, memory_init, scan,
-         r, p, q, sq, k, v, xn, sn, mn, cr, cw, dr, dq, dk, dv, dmk, dmv),
-        "gradients",
-    )
-    summed = sum_over_devices(*sums)
-    grad_query, grad_out = summed[:, :1024], summed[:, 1024:2048]
-    grad_key, grad_value = summed[:, 2048:2304], summed[:, 2304:2560]
-    grad_memory = summed[:, 2560:2688].T
-    grad_gate = summed[:, 2688]
-    place = lax.axis_index(AXES)
-
-    def mine(array):
-        return lax.dynamic_slice_in_dim(array, place * 4, 4, 0).astype(F32)
-
-    grad_gain = (
-        jnp.sum(mine(query_weight) * grad_query, axis=1)
-        + jnp.sum(mine(key_weight) * grad_key, axis=1)
-        + jnp.sum(mine(value_weight) * grad_value, axis=1)
-    ) / mine(norm_gain)
+         r, p, sq, k, v, left, mn, cr, cw, dr, dq, dk, dv, dmk, dmv),
+        "write_backward",
+    )
+    summed = sum_over_devices(
+        left, right, context, d_out, normed, pair, rest, gain, query_weight, key_weight,
+        value_weight,
+    )
+    grad_query, grad_out, grad_key, grad_value, grad_gain, grad_gate, grad_memory = local_kernel(
+        finish_kernel,
+        [((4, n), F32) for n in (1024, 1024, 256, 256)]
+        + [((1, 4), F32), ((1, 4), F32), ((128, 4), F32)],
+        (summed,),
+        "finish",
+    )
+    grad_gain, grad_gate = grad_gain[0], grad_gate[0]
     return (
         output[None, None],
         grad_query,

time: 151 us -> 140 us (0.927)
  other arithmetic: 4.27 us -> 0 us
  local copies, waits for them, and re-layouts: 4.83 us -> 1.49 us
  Pallas kernels: 140 us -> 137 us
    reduce_sum x2 -> x0, other arithmetic: 2.98 us -> none  [the longest x1 1.51 us: per_device(): jnp.sum(mine(query_weight) * grad_query, axis=1)]
    slice x2 -> x0, local copies, waits for them, and re-layouts: 2.18 us -> none  [the longest x1 1.31 us: per_device(): grad_gate = summed[:, 2688]]
    pallas_call x3 -> x4, Pallas kernels: 26.8 us -> 25.4 us  [local_kernel(): pl.pallas_call(kernel, out_shape=[jax.ShapeDtypeStruct(shape, dtype) for...]
where the time goes in v3:
time: 140 us
  Pallas kernels  137 us (98%)
  local copies, waits for them, and re-layouts  1.49 us (1%)
    pallas_call x1, Pallas kernels, sum_over_devices(): pl.pallas_call(sum_kernel, out_shape=jax.ShapeDtypeStruct((8, TOTAL + 128...  58.7 us
    pallas_call x2, Pallas kernels, entering(): pl.pallas_call(functools.partial(scan_kernel, reverse), out_shape=jax.Sha...  53.2 us
    pallas_call x4, Pallas kernels, local_kernel(): pl.pallas_call(kernel, out_shape=[jax.ShapeDtypeStruct(shape, dtype) for...  25.4 us

profile of v3, /device:TPU:32, one launch (start us, length us, event | category | flops | bytes accessed | tf_op | source)
XLA Modules:
  0.0 140.0 jit_solution(1567310034669146262)
XLA Ops:
  1.3 6.0 %write_forward.1 = (bf16[128,1024]{1,0:T(8,128)(2,1)}, bf16[128,256]{1,0:T(8,128)(2,1)}, bf16[128,256]{1,0:T(8,128)(2,1)}, bf16[256,1024]{1,0:T(8,128)(2,1)}, bf...) custom-call(s32[1,1]{1,0:T(1,128)S(6)} %copy.20.length_ref, ...), custom_call_target="tpu_custom_call" | custom-call | tf_op jit(solution)/shard_map/write_forward/pallas_call | solution.py:618
  7.3 27.9 %prefix.1.scan_ref = f32[128,1152]{1,0:T(8,128)} custom-call(f32[128,1024]{1,0:T(8,128)} %get-tuple-element.42.add_ref, f32[128,128]{1,0:T(8,128)} %get-tuple-element.43.keep_ref.retain_ref), custom_call_target="tpu_custom_call" | custom-call | tf_op jit(solution)/shard_map/prefix/pallas_call | solution.py:393
  35.2 8.7 %read_both.1 = (bf16[128,1024]{1,0:T(8,128)(2,1)}, f32[128,1024]{1,0:T(8,128)}, bf16[128,1024]{1,0:T(8,128)(2,1)}, bf16[128,1024]{1,0:T(8,128)(2,1)}, bf16[128,1...) custom-call(s32[1,1]{1,0:T(1,128)S(6)} %copy.20.length_ref, ...), custom_call_target="tpu_custom_call" | custom-call | tf_op jit(solution)/shard_map/read_both/pallas_call | solution.py:618
  43.9 25.3 %suffix.1.later_ref = f32[128,1152]{1,0:T(8,128)} custom-call(f32[128,1024]{1,0:T(8,128)} %get-tuple-element.49.add_ref.r_ref, f32[128,128]{1,0:T(8,128)} %get-tuple-element.43.keep_ref.retain_ref), custom_call_target="tpu_custom_call" | custom-call | tf_op jit(solution)/shard_map/suffix/pallas_call | solution.py:393
  69.2 9.0 %write_backward.1 = (bf16[256,1024]{1,0:T(8,128)(2,1)}, bf16[256,1024]{1,0:T(8,128)(2,1)}, bf16[256,1024]{1,0:T(8,128)(2,1)}, bf16[256,1024]{1,0:T(8,128)(2,1)},...) custom-call(f32[128,1152]{1,0:T(8,128)} %suffix.1.later_ref, f32[128,1024]{1,0:T(8,128)} %get-tuple-element.50.memory_ref, ...), custom_call_target="tpu_custom_call" | custom-call | tf_op jit(solution)/shard_map/write_backward/pallas_call | solution.py:618
  78.2 58.7 %sum_over_devices.1.full = f32[8,2944]{1,0:T(8,128)} custom-call(bf16[256,1024]{1,0:T(8,128)(2,1)} %get-tuple-element.48.left_ref.refs_0_, bf16[256,1024]{1,0:T(8,128)(2,1)} %get-tuple-element.63.refs_1_, bf16[256,1024]{1,0:T(8,128)(2,1)} %get-tuple-element.64.refs_2_, bf16[256,1024]{1,0:T(8,128)(2,1)} %get-tuple-element.65.refs_3_, ...), custom_call_target="tpu_custom_call" | custom-call | tf_op jit(solution)/shard_map/sum_over_devices/pallas_call | solution.py:281
  136.9 1.6 %finish.1 = (f32[4,1024]{1,0:T(4,128)}, f32[4,1024]{1,0:T(4,128)}, f32[4,256]{1,0:T(4,128)}, f32[4,256]{1,0:T(4,128)}, f32[1,4]{1,0:T(1,128)}, /*index=5*/f32[1,4]{1,0:T(1,128)}, f32[128,4]{1,0:T(8,128)}) custom-call(f32[8,2944]{1,0:T(8,128)} %sum_over_devices.1.full), custom_call_target="tpu_custom_call" | custom-call | tf_op jit(solution)/shard_map/finish/pallas_call | solution.py:618
  138.5 1.5 %copy.19 = f32[128,4]{0,1:T(4,128)} copy(f32[128,4]{1,0:T(8,128)} %get-tuple-element.83) | data formatting | bytes 4096

commit v4 on v3

--- a/solution.py
+++ b/solution.py
@@ -39,13 +39,6 @@
         device_id=device,
         device_id_type=MESH,
     )
-
-
-def greet(devices):
-    barrier = pltpu.get_barrier_semaphore()
-    for device in devices:
-        pl.semaphore_signal(barrier, inc=1, device_id=device, device_id_type=MESH)
-    pl.semaphore_wait(barrier, len(devices))
 
 
 class Ring:
@@ -94,20 +87,57 @@
             copy.wait_send()
 
 
+class Direct:
+    def __init__(self, axis, work, landing, out, send, receive):
+        self.work, self.landing, self.out = work, landing, out
+        self.send, self.receive = send, receive
+        self.me = place_of(axis)
+        self.steps = ((2, shift(axis, 2)), (1, shift(axis, 1)), (3, shift(axis, -1)))
+        self.copies = []
+
+    def first(self):
+        for slot, (step, device) in enumerate(self.steps):
+            copy = remote(
+                self.work.at[:, lax.rem(self.me + step, 4)],
+                self.landing.at[slot],
+                self.send.at[slot],
+                self.receive.at[slot],
+                device,
+            )
+            copy.start()
+            self.copies.append(copy)
+
+    def second(self):
+        pass
+
+    def finish(self):
+        for copy in self.copies:
+            copy.wait_recv()
+        self.out[...] = (
+            self.work[:, self.me] + self.landing[0] + self.landing[1] + self.landing[2]
+        )
+
+    def drain(self):
+        for copy in self.copies:
+            copy.wait_send()
+
+
 ORDERS = (("x", "y", "z"), ("y", "z", "x"), ("z", "x", "y"))
-WIDTHS = ((1024,), (1024,), (512, 256))
+PARTS = 6
+WIDTHS = (512, 512, 512, 512, 512, 256)
 TOTAL = 2816
 
 
 def sum_kernel(*refs):
     left, right, context, d_out, normed, pair, rest, gain, wq, wk, wv = refs[:11]
     out_ref, refs = refs[11], refs[12:]
-    products, refs = refs[:3], refs[3:]
-    landed, refs = refs[:4], refs[4:]
-    works, refs = refs[:3], refs[3:]
-    rings_of, refs = refs[:18], refs[18:]
+    products, refs = refs[:5], refs[5:]
+    landed, refs = refs[:6], refs[6:]
+    works, refs = refs[:6], refs[6:]
+    rings_of, refs = refs[:36], refs[36:]
     rows_of, refs = refs[:3], refs[3:]
-    sent, mate, fold_in, core_send, core_receive, ring_send, ring_receive, fold_sems, row_sems = refs
+    sent, mate, fold_in, refs = refs[:2], refs[2:4], refs[4:6], refs[6:]
+    core_send, core_receive, ring_send, ring_receive, fold_sems, row_sems = refs
     core = lax.axis_index("c")
     other = {"c": 1 - core}
     far = z_shift(4)
@@ -119,7 +149,8 @@
     ]
     for copy in row_copies:
         copy.start()
-    peers = [other, far] + [shift(axis, step) for axis in ("x", "y", "z") for step in (1, -1)]
+    peers = [other, far, shift("x", 2), shift("y", 2), shift("z", 2), shift("z", -2)]
+    peers += [shift(axis, step) for axis in ("x", "y", "z") for step in (1, -1)]
     barrier = pltpu.get_barrier_semaphore()
     for device in peers:
         pl.semaphore_signal(barrier, inc=1, device_id=device, device_id_type=MESH)
@@ -131,49 +162,51 @@
         copy.start()
         core_copies.append(copy)
 
-    def product(member, block, factor, other_factor):
-        value = mul_tn(factor[:, block * 256 : block * 256 + 256], other_factor[...])
-        products[member][block * 4 : block * 4 + 4] = value.reshape(4, 2, 32, value.shape[1])
-
-    def product_and_push(member, factor, other_factor):
+    def product_and_push(part):
+        factor, other_factor, start = (
+            (left, right, 0),
+            (context, d_out, 0),
+            (normed, pair, 0),
+            (left, right, 512),
+            (context, d_out, 512),
+        )[part]
         for block in range(4):
-            product(member, block, factor, other_factor)
-            if member == 0 and block == 0:
+            value = mul_tn(
+                factor[:, block * 256 : block * 256 + 256], other_factor[:, start : start + 512]
+            )
+            products[part][block * 4 : block * 4 + 4] = value.reshape(4, 2, 32, 512)
+            if part == 0 and block == 0:
                 pl.semaphore_wait(barrier, len(peers))
-                push_core(rest.at[:, 1 - core], landed[3])
-            blocks = pl.ds(block * 4, 4)
-            push_core(products[member].at[blocks, 1 - core], landed[member].at[blocks])
-
-    members = [((0, 0),), ((1, 0),), ((2, 0), (3, 512))]
+            if block % 2 == 1:
+                blocks = pl.ds((block - 1) * 4, 8)
+                push_core(products[part].at[blocks, 1 - core], landed[part].at[blocks])
+
     sources = tuple(products) + (rest,)
 
     def build_part(part):
-        order, work = ORDERS[part], works[part]
-        half_width = sum(WIDTHS[part]) // 2
+        order, work = ORDERS[part % 3], works[part]
+        half_width = WIDTHS[part] // 2
 
         def build(zl, carry):
             for x in range(4):
                 block = zl * 4 + x
-                for member, start in members[part]:
-                    for col in range(0, sources[member].shape[3], 128):
-                        cols = pl.ds(col, 128)
-                        half = (start + col) // half_width
-                        to = pl.ds((start + col) % half_width, 128)
-                        rows = (
-                            sources[member][block, core, :, cols] + landed[member][block, :, cols]
+                for col in range(0, WIDTHS[part], 128):
+                    cols = pl.ds(col, 128)
+                    half = col // half_width
+                    to = pl.ds(col % half_width, 128)
+                    rows = sources[part][block, core, :, cols] + landed[part][block, :, cols]
+                    low = lax.broadcasted_iota(jnp.int32, (8, 128), 0) < 4
+                    for pair_at in range(2):
+                        a = rows[pair_at * 8 : pair_at * 8 + 8]
+                        b = rows[16 + pair_at * 8 : 24 + pair_at * 8]
+                        tiles = (
+                            jnp.where(low, a, pltpu.roll(b, 4, 0)),
+                            jnp.where(low, pltpu.roll(a, 4, 0), b),
                         )
-                        low = lax.broadcasted_iota(jnp.int32, (8, 128), 0) < 4
-                        for pair_at in range(2):
-                            a = rows[pair_at * 8 : pair_at * 8 + 8]
-                            b = rows[16 + pair_at * 8 : 24 + pair_at * 8]
-                            tiles = (
-                                jnp.where(low, a, pltpu.roll(b, 4, 0)),
-                                jnp.where(low, pltpu.roll(a, 4, 0), b),
-                            )
-                            for bit in range(2):
-                                where = {"z": zl, "x": x, "y": pair_at * 2 + bit}
-                                index = (half,) + tuple(where[axis] for axis in order)
-                                work[index + (slice(None), to)] = tiles[bit]
+                        for bit in range(2):
+                            where = {"z": zl, "x": x, "y": pair_at * 2 + bit}
+                            index = (half,) + tuple(where[axis] for axis in order)
+                            work[index + (slice(None), to)] = tiles[bit]
             return carry
 
         lax.fori_loop(0, 4, build, 0)
@@ -188,8 +221,8 @@
         for stage in range(3):
             n = part * 3 + stage
             stages.append(
-                Ring(
-                    ORDERS[part][stage],
+                (Direct if stage else Ring)(
+                    ORDERS[part % 3][stage],
                     works[part] if stage == 0 else rings_of[2 * (n - 1) + 1],
                     rings_of[2 * n],
                     rings_of[2 * n + 1],
@@ -200,34 +233,61 @@
         rings.append(stages)
         stages[0].first()
 
-    product_and_push(0, left, right)
-    product_and_push(1, context, d_out)
-    begin(0, (1, 2, 3, 4))
-    product_and_push(2, normed, pair)
-    begin(1, (5, 6, 7, 8))
-    begin(2, (0, 9, 10, 11, 12))
-    for stage in range(3):
-        for part in range(3):
+    early, late = (0, 1, 2), (3, 4, 5)
+
+    def second(parts, stage):
+        for part in parts:
             rings[part][stage].second()
-        for part in range(3):
+
+    def finish(parts, stage):
+        for part in parts:
             rings[part][stage].finish()
             if stage < 2:
                 rings[part][stage + 1].first()
-    total = jnp.concatenate(
-        [rings_of[2 * (part * 3 + 2) + 1][half] for part in range(3) for half in range(2)], axis=1
-    )
-    turned = pltpu.roll(total, 4, 0)
+
     high = lax.axis_index("zh")
-    fold = lax.broadcasted_iota(jnp.int32, (8, TOTAL // 2), 0) < 4
-
-    def folded(upright, upside):
-        return jnp.where(fold, upright[:, : TOTAL // 2], upside[:, TOTAL // 2 :])
-
-    straight, crossed = folded(total, turned), folded(turned, total)
-    sent[...] = jnp.where(high == 1, straight, crossed)
-    mate[...] = jnp.where(high == 0, straight, crossed)
-    last = remote(sent, fold_in, fold_sems.at[0], fold_sems.at[1], far)
-    last.start()
+    folds = []
+
+    def fold(parts, which):
+        total = jnp.concatenate(
+            [rings_of[2 * (part * 3 + 2) + 1][half] for part in parts for half in range(2)],
+            axis=1,
+        )
+        turned = pltpu.roll(total, 4, 0)
+        middle = total.shape[1] // 2
+        top = lax.broadcasted_iota(jnp.int32, (8, middle), 0) < 4
+        straight = jnp.where(top, total[:, :middle], turned[:, middle:])
+        crossed = jnp.where(top, turned[:, :middle], total[:, middle:])
+        sent[which][...] = jnp.where(high == 1, straight, crossed)
+        mate[which][...] = jnp.where(high == 0, straight, crossed)
+        copy = remote(
+            sent[which], fold_in[which], fold_sems.at[which, 0], fold_sems.at[which, 1], far
+        )
+        copy.start()
+        folds.append(copy)
+
+    product_and_push(0)
+    product_and_push(1)
+    product_and_push(2)
+    begin(0, (0, 1))
+    product_and_push(3)
+    begin(1, (2, 3))
+    product_and_push(4)
+    begin(2, (4, 5))
+    push_core(rest.at[:, 1 - core], landed[5])
+    begin(3, (6, 7))
+    second(early, 0)
+    begin(4, (8, 9))
+    begin(5, (10,))
+    finish(early, 0)
+    second(late, 0)
+    finish(early, 1)
+    finish(late, 0)
+    finish(early, 2)
+    fold(early, 0)
+    finish(late, 1)
+    finish(late, 2)
+    fold(late, 1)
     for copy in core_copies:
         copy.wait_send()
     for stages in rings:
@@ -246,36 +306,39 @@
     low = lax.broadcasted_iota(jnp.int32, (8, 1), 0) < 4
     gains = jnp.sum(jnp.where(here, gain[...], 0.0), axis=1, keepdims=True)
     gains = jnp.where(low, gains, 1.0)
-    last.wait()
-    short = mate[...] + fold_in[...]
-    full = jnp.concatenate([short, pltpu.roll(short, 4, 0)], axis=1)
+    pieces = []
+    for which in range(2):
+        folds[which].wait()
+        short = mate[which][...] + fold_in[which][...]
+        pieces += [short, pltpu.roll(short, 4, 0)]
+    full = jnp.concatenate(pieces, axis=1)
     of_gain = (
-        jnp.sum(weights[0] * full[:, :1024], axis=1, keepdims=True)
-        + jnp.sum(weights[1] * full[:, 2048:2304], axis=1, keepdims=True)
-        + jnp.sum(weights[2] * full[:, 2304:2560], axis=1, keepdims=True)
+        jnp.sum(weights[0][:, :512] * full[:, :512], axis=1, keepdims=True)
+        + jnp.sum(weights[0][:, 512:] * full[:, 1536:2048], axis=1, keepdims=True)
+        + jnp.sum(weights[1] * full[:, 1024:1280], axis=1, keepdims=True)
+        + jnp.sum(weights[2] * full[:, 1280:1536], axis=1, keepdims=True)
     ) / gains
     out_ref[:, :TOTAL] = full
     out_ref[:, TOTAL:] = jnp.broadcast_to(of_gain, (8, 128))
 
 
 def sum_over_devices(left, right, context, d_out, normed, pair, rest, gain, wq, wk, wv):
-    widths = (1024, 1024, 512, 256)
-    scratch = [pltpu.VMEM((16, 2, 32, n), F32) for n in widths[:3]]
-    scratch += [pltpu.VMEM((16, 32, n), F32) for n in widths]
-    halves = [sum(w) // 2 for w in WIDTHS]
-    scratch += [pltpu.VMEM((2, 4, 4, 4, 8, n), F32) for n in halves]
-    for n in halves:
+    scratch = [pltpu.VMEM((16, 2, 32, n), F32) for n in WIDTHS[:5]]
+    scratch += [pltpu.VMEM((16, 32, n), F32) for n in WIDTHS]
+    scratch += [pltpu.VMEM((2, 4, 4, 4, 8, n // 2), F32) for n in WIDTHS]
+    for n in WIDTHS:
         for stage in range(3):
-            tail = (4,) * (2 - stage) + (8, n)
-            scratch += [pltpu.VMEM((6,) + tail, F32), pltpu.VMEM((2,) + tail, F32)]
+            tail = (4,) * (2 - stage) + (8, n // 2)
+            lands = (3, 2) if stage else (6,)
+            scratch += [pltpu.VMEM(lands + tail, F32), pltpu.VMEM((2,) + tail, F32)]
     scratch += [pltpu.VMEM((16, n), BF16) for n in (1024, 256, 256)]
-    scratch += [pltpu.VMEM((8, TOTAL // 2), F32)] * 3
+    scratch += [pltpu.VMEM((8, n), F32) for n in (768, 640)] * 3
     scratch += [
-        pltpu.SemaphoreType.DMA((13,)),
-        pltpu.SemaphoreType.DMA((13,)),
-        pltpu.SemaphoreType.DMA((9, 6)),
-        pltpu.SemaphoreType.DMA((9, 6)),
-        pltpu.SemaphoreType.DMA((2,)),
+        pltpu.SemaphoreType.DMA((11,)),
+        pltpu.SemaphoreType.DMA((11,)),
+        pltpu.SemaphoreType.DMA((18, 6)),
+        pltpu.SemaphoreType.DMA((18, 6)),
+        pltpu.SemaphoreType.DMA((2, 2)),
         pltpu.SemaphoreType.DMA((3,)),
     ]
     return pl.pallas_call(
@@ -292,12 +355,13 @@
 
 
 def finish_kernel(full, gq, go, gk, gv, gain, gate, memory):
-    gq[...] = full[:4, :1024]
-    go[...] = full[:4, 1024:2048]
-    gk[...] = full[:4, 2048:2304]
-    gv[...] = full[:4, 2304:2560]
-    rows = jnp.concatenate([full[:, 2560:2688]] + [jnp.zeros((120, 128), F32)], axis=0)
-    memory[...] = jnp.transpose(rows)[:, :4]
+    gq[:, :512] = full[:4, :512]
+    gq[:, 512:] = full[:4, 1536:2048]
+    go[:, :512] = full[:4, 512:1024]
+    go[:, 512:] = full[:4, 2048:2560]
+    gk[...] = full[:4, 1024:1280]
+    gv[...] = full[:4, 1280:1536]
+    memory[...] = full[:4, 2560:2688]
     for ref, start in ((gate, 2688), (gain, TOTAL)):
         rows = jnp.concatenate([full[:, start : start + 128], jnp.zeros((120, 128), F32)], axis=0)
         ref[...] = jnp.transpose(rows)[:1, :4]
@@ -319,72 +383,100 @@
     )
 
 
-def scan_kernel(reverse, add_ref, keep_ref, out_ref, own, mate, pair, xs, zs, backs, down, up, far, send, receive):
+CHUNKS = 2
+CORE_ROWS, X_ROWS = 32, 8
+
+
+def scan_kernel(
+    reverse, add_ref, keep_ref, out_ref, own, mate, pair, xs, zs, backs, down, up, far, send,
+    receive,
+):
     core, x, zl = lax.axis_index("c"), lax.axis_index("x"), lax.axis_index("zl")
     other = {"c": 1 - core}
     x_peers = [{"x": lax.rem(x + k, 4)} for k in (1, 2, 3)]
     z_peers = [{"zl": lax.rem(zl + k, 4)} for k in (1, 2, 3)]
+    peers = [other] + x_peers + z_peers
+    barrier = pltpu.get_barrier_semaphore()
+    for device in peers:
+        pl.semaphore_signal(barrier, inc=1, device_id=device, device_id_type=MESH)
     own[:, :1024] = add_ref[...]
     own[:, 1024:] = keep_ref[...]
-    greet([other] + x_peers + z_peers)
-
-    def rows_of(start, count):
-        return pl.ds(pl.multiple_of(start, count), count)
-
-    mine = rows_of(core * 64, 64)
-    theirs = rows_of((1 - core) * 64, 64)
-    copies = []
-
-    def push(source, target, device):
-        n = len(copies)
-        copy = remote(source, target, send.at[n], receive.at[n], device)
-        copy.start()
-        copies.append(copy)
-        return copy
-
-    push(own.at[theirs], mate, other).wait_recv()
+    pl.semaphore_wait(barrier, len(peers))
+    order = (3, 2, 1, 0) if reverse else (0, 1, 2, 3)
     leads = core == (1 if reverse else 0)
-    kept, got = own[mine], mate[...]
-    earlier = jnp.where(leads, kept, got)
-    pair[...] = joined(earlier, jnp.where(leads, got, kept))
-    started = [
-        push(pair.at[rows_of(lax.rem(x + k, 4) * 16, 16)], xs.at[x], x_peers[k - 1])
-        for k in (1, 2, 3)
-    ]
-    xs[x] = pair[rows_of(x * 16, 16)]
-    for copy in started:
-        copy.wait_recv()
-    order = (3, 2, 1, 0) if reverse else (0, 1, 2, 3)
-    inside = {}
-    running = None
-    for k in order:
-        inside[k] = running
-        running = xs[k] if running is None else joined(running, xs[k])
-    zs[zl] = running
-    started = [push(zs.at[zl], zs.at[zl], z_peers[k - 1]) for k in (1, 2, 3)]
-    for copy in started:
-        copy.wait_recv()
-    before = identity_rows(16)
-    for k in order[:3]:
-        passed = k > zl if reverse else k < zl
-        before = jnp.where(passed, joined(before, zs[k]), before)
-    for k in order:
-        backs[k] = before if inside[k] is None else joined(before, inside[k])
-    started = [
-        push(backs.at[lax.rem(x + k, 4)], down.at[rows_of(x * 16, 16)], x_peers[k - 1])
-        for k in (1, 2, 3)
-    ]
-    down[rows_of(x * 16, 16)] = backs[x]
-    for copy in started:
-        copy.wait_recv()
-    lead = down[...]
-    follow = joined(lead, earlier)
-    up[...] = jnp.where(leads, follow, lead)
-    last = push(up, far, other)
-    out_ref[mine] = jnp.where(leads, lead, follow)
-    last.wait_recv()
-    out_ref[theirs] = far[...]
-    for copy in copies:
+    all_copies = []
+
+    def chunk_of(chunk):
+        copies = []
+
+        def push(source, target, device):
+            n = len(copies)
+            copy = remote(source, target, send.at[chunk, n], receive.at[chunk, n], device)
+            copy.start()
+            copies.append(copy)
+            all_copies.append(copy)
+            return copy
+
+        def rows_of(start, count):
+            return pl.ds(pl.multiple_of(start, count), count)
+
+        mine = rows_of(chunk * 2 * CORE_ROWS + core * CORE_ROWS, CORE_ROWS)
+        theirs = rows_of(chunk * 2 * CORE_ROWS + (1 - core) * CORE_ROWS, CORE_ROWS)
+        at_x = [rows_of(lax.rem(x + k, 4) * X_ROWS, X_ROWS) for k in range(4)]
+        started = push(own.at[theirs], mate.at[chunk], other)
+        yield
+        started.wait_recv()
+        kept, got = own[mine], mate[chunk]
+        earlier = jnp.where(leads, kept, got)
+        pair[chunk] = joined(earlier, jnp.where(leads, got, kept))
+        started = [
+            push(pair.at[chunk, at_x[k]], xs.at[chunk, x], x_peers[k - 1]) for k in (2, 1, 3)
+        ]
+        xs[chunk, x] = pair[chunk, at_x[0]]
+        yield
+        for copy in started:
+            copy.wait_recv()
+        inside = {}
+        running = None
+        for k in order:
+            inside[k] = running
+            running = xs[chunk, k] if running is None else joined(running, xs[chunk, k])
+        zs[chunk, zl] = running
+        started = [
+            push(zs.at[chunk, zl], zs.at[chunk, zl], z_peers[k - 1])
+            for k in ((1, 2, 3) if reverse else (3, 2, 1))
+        ]
+        yield
+        for copy in started:
+            copy.wait_recv()
+        before = identity_rows(X_ROWS)
+        for k in order[:3]:
+            passed = k > zl if reverse else k < zl
+            before = jnp.where(passed, joined(before, zs[chunk, k]), before)
+        for k in order:
+            backs[chunk, k] = before if inside[k] is None else joined(before, inside[k])
+        started = [
+            push(backs.at[chunk, lax.rem(x + k, 4)], down.at[chunk, at_x[0]], x_peers[k - 1])
+            for k in (2, 1, 3)
+        ]
+        down[chunk, at_x[0]] = backs[chunk, x]
+        yield
+        for copy in started:
+            copy.wait_recv()
+        lead = down[chunk]
+        follow = joined(lead, earlier)
+        up[chunk] = jnp.where(leads, follow, lead)
+        started = push(up.at[chunk], far.at[chunk], other)
+        out_ref[mine] = jnp.where(leads, lead, follow)
+        yield
+        started.wait_recv()
+        out_ref[theirs] = far[chunk]
+
+    running = [chunk_of(chunk) for chunk in range(CHUNKS)]
+    for step in range(6):
+        for steps in running:
+            next(steps, None)
+    for copy in all_copies:
         copy.wait_send()
 
 
@@ -397,16 +489,16 @@
         out_specs=VMEM_SPEC,
         scratch_shapes=[
             pltpu.VMEM((128, WIDE), f32),
-            pltpu.VMEM((64, WIDE), f32),
-            pltpu.VMEM((64, WIDE), f32),
-            pltpu.VMEM((4, 16, WIDE), f32),
-            pltpu.VMEM((4, 16, WIDE), f32),
-            pltpu.VMEM((4, 16, WIDE), f32),
-            pltpu.VMEM((64, WIDE), f32),
-            pltpu.VMEM((64, WIDE), f32),
-            pltpu.VMEM((64, WIDE), f32),
-            pltpu.SemaphoreType.DMA((11,)),
-            pltpu.SemaphoreType.DMA((11,)),
+            pltpu.VMEM((CHUNKS, CORE_ROWS, WIDE), f32),
+            pltpu.VMEM((CHUNKS, CORE_ROWS, WIDE), f32),
+            pltpu.VMEM((CHUNKS, 4, X_ROWS, WIDE), f32),
+            pltpu.VMEM((CHUNKS, 4, X_ROWS, WIDE), f32),
+            pltpu.VMEM((CHUNKS, 4, X_ROWS, WIDE), f32),
+            pltpu.VMEM((CHUNKS, CORE_ROWS, WIDE), f32),
+            pltpu.VMEM((CHUNKS, CORE_ROWS, WIDE), f32),
+            pltpu.VMEM((CHUNKS, CORE_ROWS, WIDE), f32),
+            pltpu.SemaphoreType.DMA((CHUNKS, 11)),
+            pltpu.SemaphoreType.DMA((CHUNKS, 11)),
         ],
         compiler_params=pltpu.CompilerParams(
             collective_id=1 if reverse else 0, has_side_effects=True
@@ -673,11 +765,11 @@
     grad_query, grad_out, grad_key, grad_value, grad_gain, grad_gate, grad_memory = local_kernel(
         finish_kernel,
         [((4, n), F32) for n in (1024, 1024, 256, 256)]
-        + [((1, 4), F32), ((1, 4), F32), ((128, 4), F32)],
+        + [((1, 4), F32), ((1, 4), F32), ((4, 128), F32)],
         (summed,),
         "finish",
     )
-    grad_gain, grad_gate = grad_gain[0], grad_gate[0]
+    grad_gain, grad_gate, grad_memory = grad_gain[0], grad_gate[0], grad_memory.T
     return (
         output[None, None],
         grad_query,

time: 140 us -> 130 us (0.929); the launches traced: 140 us -> 128 us
  Pallas kernels: 137 us -> 127 us
  local copies, waits for them, and re-layouts: 1.49 us -> 0 us
    pallas_call x2, Pallas kernels: 53.2 us -> 47.9 us  [entering(): pl.pallas_call(functools.partial(scan_kernel, reverse), out_shape=jax.Sha...]
    pallas_call x1, Pallas kernels: 58.7 us -> 53.7 us  [sum_over_devices(): pl.pallas_call(sum_kernel, out_shape=jax.ShapeDtypeStruct((8, TOTAL + 128...]
    unnamed x1 -> x0, local copies, waits for them, and re-layouts: 1.49 us -> none
where the time goes in v4:
time: 130 us; the launch traced here: 128 us
  Pallas kernels  127 us (98%)
  between operations  1.31 us (1%)
    pallas_call x1, Pallas kernels, sum_over_devices(): pl.pallas_call(sum_kernel, out_shape=jax.ShapeDtypeStruct((8, TOTAL + 128...  53.7 us
    pallas_call x2, Pallas kernels, entering(): pl.pallas_call(functools.partial(scan_kernel, reverse), out_shape=jax.Sha...  47.9 us
    pallas_call x4, Pallas kernels, local_kernel(): pl.pallas_call(kernel, out_shape=[jax.ShapeDtypeStruct(shape, dtype) for...  25.3 us

profile of v4, /device:TPU:32, one launch (start us, length us, event | category | flops | bytes accessed | tf_op | source)
XLA Modules:
  0.0 128.2 jit_solution(4766693653403956461)
XLA Ops:
  1.3 6.0 %write_forward.1 = (bf16[128,1024]{1,0:T(8,128)(2,1)}, bf16[128,256]{1,0:T(8,128)(2,1)}, bf16[128,256]{1,0:T(8,128)(2,1)}, bf16[256,1024]{1,0:T(8,128)(2,1)}, bf...) custom-call(s32[1,1]{1,0:T(1,128)S(6)} %copy.19.length_ref, ...), custom_call_target="tpu_custom_call" | custom-call | tf_op jit(solution)/shard_map/write_forward/pallas_call | solution.py:710
  7.3 24.4 %prefix.1.scan_ref = f32[128,1152]{1,0:T(8,128)} custom-call(f32[128,1024]{1,0:T(8,128)} %get-tuple-element.42.add_ref, f32[128,128]{1,0:T(8,128)} %get-tuple-element.43.keep_ref.retain_ref), custom_call_target="tpu_custom_call" | custom-call | tf_op jit(solution)/shard_map/prefix/pallas_call | solution.py:485
  31.7 8.7 %read_both.1 = (bf16[128,1024]{1,0:T(8,128)(2,1)}, f32[128,1024]{1,0:T(8,128)}, bf16[128,1024]{1,0:T(8,128)(2,1)}, bf16[128,1024]{1,0:T(8,128)(2,1)}, bf16[128,1...) custom-call(s32[1,1]{1,0:T(1,128)S(6)} %copy.19.length_ref, ...), custom_call_target="tpu_custom_call" | custom-call | tf_op jit(solution)/shard_map/read_both/pallas_call | solution.py:710
  40.4 23.5 %suffix.1.later_ref = f32[128,1152]{1,0:T(8,128)} custom-call(f32[128,1024]{1,0:T(8,128)} %get-tuple-element.49.add_ref.r_ref, f32[128,128]{1,0:T(8,128)} %get-tuple-element.43.keep_ref.retain_ref), custom_call_target="tpu_custom_call" | custom-call | tf_op jit(solution)/shard_map/suffix/pallas_call | solution.py:485
  63.9 9.0 %write_backward.1 = (bf16[256,1024]{1,0:T(8,128)(2,1)}, bf16[256,1024]{1,0:T(8,128)(2,1)}, bf16[256,1024]{1,0:T(8,128)(2,1)}, bf16[256,1024]{1,0:T(8,128)(2,1)},...) custom-call(f32[128,1152]{1,0:T(8,128)} %suffix.1.later_ref, f32[128,1024]{1,0:T(8,128)} %get-tuple-element.50.memory_ref, ...), custom_call_target="tpu_custom_call" | custom-call | tf_op jit(solution)/shard_map/write_backward/pallas_call | solution.py:710
  72.9 53.7 %sum_over_devices.1.full = f32[8,2944]{1,0:T(8,128)} custom-call(bf16[256,1024]{1,0:T(8,128)(2,1)} %get-tuple-element.48.left_ref.refs_0_, bf16[256,1024]{1,0:T(8,128)(2,1)} %get-tuple-element.63.refs_1_, bf16[256,1024]{1,0:T(8,128)(2,1)} %get-tuple-element.64.refs_2_, bf16[256,1024]{1,0:T(8,128)(2,1)} %get-tuple-element.65.refs_3_, ...), custom_call_target="tpu_custom_call" | custom-call | tf_op jit(solution)/shard_map/sum_over_devices/pallas_call | solution.py:344
  126.7 1.5 %finish.1 = (f32[4,1024]{1,0:T(4,128)}, f32[4,1024]{1,0:T(4,128)}, f32[4,256]{1,0:T(4,128)}, f32[4,256]{1,0:T(4,128)}, f32[1,4]{1,0:T(1,128)}, /*index=5*/f32[1,4]{1,0:T(1,128)}, f32[4,128]{1,0:T(4,128)}) custom-call(f32[8,2944]{1,0:T(8,128)} %sum_over_devices.1.full), custom_call_target="tpu_custom_call" | custom-call | tf_op jit(solution)/shard_map/finish/pallas_call | solution.py:710

commit v5 on v4

--- a/solution.py
+++ b/solution.py
@@ -129,13 +129,18 @@
 
 
 def sum_kernel(*refs):
-    left, right, context, d_out, normed, pair, rest, gain, wq, wk, wv = refs[:11]
-    out_ref, refs = refs[11], refs[12:]
+    (
+        later_ref, memory_ref, written_ref, retain_ref, vector_ref, wq_ref, wo_ref, gain,
+        start_ref, scan_ref, r_ref, p_ref, sq_ref, k_ref, v_ref, left, mn_ref,
+        cr_ref, cw_ref, dr_ref, dq_ref, dk_ref, dv_ref, dmk_ref, dmv_ref, wk, wv,
+    ) = refs[:27]
+    out_ref, refs = refs[27], refs[28:]
+    right, context, d_out, normed, pair, rest, *refs = refs
     products, refs = refs[:5], refs[5:]
     landed, refs = refs[:6], refs[6:]
     works, refs = refs[:6], refs[6:]
     rings_of, refs = refs[:36], refs[36:]
-    rows_of, refs = refs[:3], refs[3:]
+    rows_of, refs = refs[:2], refs[2:]
     sent, mate, fold_in, refs = refs[:2], refs[2:4], refs[4:6], refs[6:]
     core_send, core_receive, ring_send, ring_receive, fold_sems, row_sems = refs
     core = lax.axis_index("c")
@@ -145,7 +150,7 @@
     base = pl.ds(pl.multiple_of(lax.div(place, 4) * 16, 16), 16)
     row_copies = [
         pltpu.make_async_copy(w.at[base], rows, row_sems.at[k])
-        for k, (w, rows) in enumerate(zip((wq, wk, wv), rows_of))
+        for k, (w, rows) in enumerate(zip((wk, wv), rows_of))
     ]
     for copy in row_copies:
         copy.start()
@@ -155,12 +160,14 @@
     for device in peers:
         pl.semaphore_signal(barrier, inc=1, device_id=device, device_id_type=MESH)
     core_copies = []
-
-    def push_core(source, target):
+    core_of = {}
+
+    def push_core(part, source, target):
         n = len(core_copies)
         copy = remote(source, target, core_send.at[n], core_receive.at[n], other)
         copy.start()
         core_copies.append(copy)
+        core_of.setdefault(part, []).append(copy)
 
     def product_and_push(part):
         factor, other_factor, start = (
@@ -175,11 +182,11 @@
                 factor[:, block * 256 : block * 256 + 256], other_factor[:, start : start + 512]
             )
             products[part][block * 4 : block * 4 + 4] = value.reshape(4, 2, 32, 512)
-            if part == 0 and block == 0:
+            if not core_copies and block == 0:
                 pl.semaphore_wait(barrier, len(peers))
             if block % 2 == 1:
                 blocks = pl.ds((block - 1) * 4, 8)
-                push_core(products[part].at[blocks, 1 - core], landed[part].at[blocks])
+                push_core(part, products[part].at[blocks, 1 - core], landed[part].at[blocks])
 
     sources = tuple(products) + (rest,)
 
@@ -211,11 +218,11 @@
 
         lax.fori_loop(0, 4, build, 0)
 
-    rings = []
-
-    def begin(part, waited):
-        for n in waited:
-            core_copies[n].wait_recv()
+    rings = {}
+
+    def begin(part):
+        for copy in core_of[part]:
+            copy.wait_recv()
         build_part(part)
         stages = []
         for stage in range(3):
@@ -230,7 +237,7 @@
                     ring_receive.at[n],
                 )
             )
-        rings.append(stages)
+        rings[part] = stages
         stages[0].first()
 
     early, late = (0, 1, 2), (3, 4, 5)
@@ -266,39 +273,90 @@
         copy.start()
         folds.append(copy)
 
+    later = later_ref[:, :1024]
+    written = written_ref[...]
+    retain = retain_ref[:, :1]
+    d_retain = jnp.sum(later * (memory_ref[...] - written), axis=-1, keepdims=True)
+    d_logit = d_retain * retain * (1.0 - retain)
+    gate = jnp.sum(written * d_logit, axis=0, keepdims=True)
+    d_written = ((1.0 - retain) * later + d_logit * vector_ref[...]).astype(BF16)
+    context[:SEG] = cr_ref[...]
+    context[SEG:] = cw_ref[...]
+    d_out[:SEG] = dr_ref[...]
+    d_out[SEG:] = d_written
+    product_and_push(1)
+    product_and_push(4)
+    begin(1)
+    begin(4)
+    d_context = mul_nt(d_written, wo_ref[...]).astype(BF16)
+    slots, keys, values = sq_ref[...], k_ref[...], v_ref[...]
+    d_slots, d_keys, d_values = [], [], []
+    for group in range(GROUPS):
+        rounded = p_ref[group]
+        dq, dk, dv = attend_back(
+            rounded.astype(F32), rounded, stacked(slots, group), of_group(keys, group),
+            of_group(values, group), stacked(d_context, group),
+        )
+        d_slots.append(side_by_side(dq))
+        d_keys.append(dk.astype(BF16))
+        d_values.append(dv.astype(BF16))
+
+    def added(one, two):
+        return (one.astype(F32) + two.astype(F32)).astype(BF16)
+
+    scale = jnp.asarray(score_scale, BF16)
+    d_slot = jnp.concatenate(d_slots, axis=1) * scale
+    right[:SEG] = dq_ref[...] * scale
+    right[SEG:] = d_slot
     product_and_push(0)
-    product_and_push(1)
+    product_and_push(3)
+    second((1,), 0)
+    begin(0)
+    pair[:SEG, :256] = added(dk_ref[...], jnp.concatenate(d_keys, axis=1))
+    pair[:SEG, 256:] = added(dv_ref[...], jnp.concatenate(d_values, axis=1))
+    pair[SEG:, :256] = dmk_ref[...]
+    pair[SEG:, 256:] = dmv_ref[...]
+    normed[:SEG] = left[:SEG]
+    normed[SEG:] = mn_ref[...]
     product_and_push(2)
-    begin(0, (0, 1))
-    product_and_push(3)
-    begin(1, (2, 3))
-    product_and_push(4)
-    begin(2, (4, 5))
-    push_core(rest.at[:, 1 - core], landed[5])
-    begin(3, (6, 7))
-    second(early, 0)
-    begin(4, (8, 9))
-    begin(5, (10,))
-    finish(early, 0)
-    second(late, 0)
-    finish(early, 1)
-    finish(late, 0)
-    finish(early, 2)
+    begin(3)
+    begin(2)
+    second((4, 0), 0)
+    d_sn = mul_nt(d_slot, wq_ref[...]).astype(BF16).astype(F32)
+    start = start_ref[...].astype(F32)
+    total = normalize_back(start, gain[...], d_sn) + scan_ref[:, 1024:1025] * r_ref[...]
+    gates = jnp.broadcast_to(gate, (128, 1024))
+    for block in range(8):
+        rows = slice(block * 128, block * 128 + 128)
+        blocks = slice(block * 2, block * 2 + 2)
+        rest[blocks, :, :, :128] = jnp.transpose(total[:, rows]).reshape(2, 2, 32, 128)
+        rest[blocks, :, :, 128:] = jnp.transpose(gates[:, rows]).reshape(2, 2, 32, 128)
+    push_core(5, rest.at[:, 1 - core], landed[5])
+    second((2,), 0)
+    begin(5)
+    finish((1,), 0)
+    second((3,), 0)
+    finish((0, 2), 0)
+    second((5,), 0)
+    finish((4,), 0)
+    finish((1, 0, 2), 1)
+    finish((3, 5), 0)
+    finish((1, 0, 2), 2)
     fold(early, 0)
-    finish(late, 1)
-    finish(late, 2)
+    finish((4, 5, 3), 1)
+    finish((4, 5, 3), 2)
     fold(late, 1)
     for copy in core_copies:
         copy.wait_send()
-    for stages in rings:
+    for stages in rings.values():
         for ring in stages:
             ring.drain()
     for copy in row_copies:
         copy.wait()
     part_of_16 = lax.rem(place, 4)
     weights = []
-    for rows in rows_of:
-        loaded = rows[...].astype(F32)
+    for loaded in (wq_ref[base], rows_of[0][...], rows_of[1][...]):
+        loaded = loaded.astype(F32)
         tile = jnp.where(part_of_16 >= 2, loaded[8:], loaded[:8])
         weights.append(jnp.where(lax.rem(place, 2) == 1, pltpu.roll(tile, 4, 0), tile))
     spot = place * 4 + lax.broadcasted_iota(jnp.int32, (8, 1024), 0)
@@ -322,8 +380,10 @@
     out_ref[:, TOTAL:] = jnp.broadcast_to(of_gain, (8, 128))
 
 
-def sum_over_devices(left, right, context, d_out, normed, pair, rest, gain, wq, wk, wv):
-    scratch = [pltpu.VMEM((16, 2, 32, n), F32) for n in WIDTHS[:5]]
+def sum_over_devices(*operands):
+    tall = pltpu.VMEM((2 * SEG, 1024), BF16)
+    scratch = [tall] * 4 + [pltpu.VMEM((2 * SEG, 512), BF16), pltpu.VMEM((16, 2, 32, 256), F32)]
+    scratch += [pltpu.VMEM((16, 2, 32, n), F32) for n in WIDTHS[:5]]
     scratch += [pltpu.VMEM((16, 32, n), F32) for n in WIDTHS]
     scratch += [pltpu.VMEM((2, 4, 4, 4, 8, n // 2), F32) for n in WIDTHS]
     for n in WIDTHS:
@@ -331,7 +391,7 @@
             tail = (4,) * (2 - stage) + (8, n // 2)
             lands = (3, 2) if stage else (6,)
             scratch += [pltpu.VMEM(lands + tail, F32), pltpu.VMEM((2,) + tail, F32)]
-    scratch += [pltpu.VMEM((16, n), BF16) for n in (1024, 256, 256)]
+    scratch += [pltpu.VMEM((16, n), BF16) for n in (256, 256)]
     scratch += [pltpu.VMEM((8, n), F32) for n in (768, 640)] * 3
     scratch += [
         pltpu.SemaphoreType.DMA((11,)),
@@ -344,14 +404,14 @@
     return pl.pallas_call(
         sum_kernel,
         out_shape=jax.ShapeDtypeStruct((8, TOTAL + 128), F32),
-        in_specs=[VMEM_SPEC] * 8 + [pl.BlockSpec(memory_space=pl.ANY)] * 3,
+        in_specs=[VMEM_SPEC] * 25 + [pl.BlockSpec(memory_space=pl.ANY)] * 2,
         out_specs=VMEM_SPEC,
         scratch_shapes=scratch,
         compiler_params=pltpu.CompilerParams(
             collective_id=2, has_side_effects=True, vmem_limit_bytes=60 << 20
         ),
         name="sum_over_devices",
-    )(left, right, context, d_out, normed, pair, rest.reshape(16, 2, 32, 256), gain, wq, wk, wv)
+    )(*operands)
 
 
 def finish_kernel(full, gq, go, gk, gv, gain, gate, memory):
@@ -652,59 +712,6 @@
     r_ref[...] = normalize_back(memory, gain, d_mn.astype(BF16).astype(F32))
 
 
-def back_kernel(
-    later_ref, memory_ref, written_ref, retain_ref, vector_ref, wq_ref, wo_ref, gain_ref,
-    start_ref, scan_ref, r_ref, p_ref, sq_ref, k_ref, v_ref, left_ref, mn_ref,
-    cr_ref, cw_ref, dr_ref, dq_ref, dk_ref, dv_ref, dmk_ref, dmv_ref,
-    right_ref, context_ref, dout_ref, normed_ref, pair_ref, rest_ref,
-):
-    later = later_ref[:, :1024]
-    written = written_ref[...]
-    retain = retain_ref[:, :1]
-    d_retain = jnp.sum(later * (memory_ref[...] - written), axis=-1, keepdims=True)
-    d_logit = d_retain * retain * (1.0 - retain)
-    gate = jnp.sum(written * d_logit, axis=0, keepdims=True)
-    d_written = ((1.0 - retain) * later + d_logit * vector_ref[...]).astype(BF16)
-    d_context = mul_nt(d_written, wo_ref[...]).astype(BF16)
-    slots, keys, values = sq_ref[...], k_ref[...], v_ref[...]
-    d_slots, d_keys, d_values = [], [], []
-    for group in range(GROUPS):
-        rounded = p_ref[group]
-        dq, dk, dv = attend_back(
-            rounded.astype(F32), rounded, stacked(slots, group), of_group(keys, group),
-            of_group(values, group), stacked(d_context, group),
-        )
-        d_slots.append(side_by_side(dq))
-        d_keys.append(dk.astype(BF16))
-        d_values.append(dv.astype(BF16))
-
-    def added(first, second):
-        return (first.astype(F32) + second.astype(F32)).astype(BF16)
-
-    scale = jnp.asarray(score_scale, BF16)
-    d_slot = jnp.concatenate(d_slots, axis=1) * scale
-    right_ref[:SEG] = dq_ref[...] * scale
-    right_ref[SEG:] = d_slot
-    pair_ref[:SEG, :256] = added(dk_ref[...], jnp.concatenate(d_keys, axis=1))
-    pair_ref[:SEG, 256:] = added(dv_ref[...], jnp.concatenate(d_values, axis=1))
-    pair_ref[SEG:, :256] = dmk_ref[...]
-    pair_ref[SEG:, 256:] = dmv_ref[...]
-    normed_ref[:SEG] = left_ref[:SEG]
-    normed_ref[SEG:] = mn_ref[...]
-    context_ref[:SEG] = cr_ref[...]
-    context_ref[SEG:] = cw_ref[...]
-    dout_ref[:SEG] = dr_ref[...]
-    dout_ref[SEG:] = d_written
-    d_sn = mul_nt(d_slot, wq_ref[...]).astype(BF16).astype(F32)
-    start = start_ref[...].astype(F32)
-    total = normalize_back(start, gain_ref[...], d_sn) + scan_ref[:, 1024:1025] * r_ref[...]
-    gates = jnp.broadcast_to(gate, (128, 1024))
-    for block in range(8):
-        rows = slice(block * 128, block * 128 + 128)
-        rest_ref[rows, :128] = jnp.transpose(total[:, rows])
-        rest_ref[rows, 128:] = jnp.transpose(gates[:, rows])
-
-
 def local_kernel(kernel, shapes, operands, name):
     smem = pl.BlockSpec(memory_space=pltpu.SMEM)
     return pl.pallas_call(
@@ -751,16 +758,9 @@
         "read_both",
     )
     later = entering(retain, r, True)
-    right, context, d_out, normed, pair, rest = local_kernel(
-        back_kernel,
-        [double, double, double, double, ((2 * SEG, 512), BF16), ((1024, 256), F32)],
-        (later, memory, written, retain, vector, query_weight, out_weight, gain, memory_init, scan,
-         r, p, sq, k, v, left, mn, cr, cw, dr, dq, dk, dv, dmk, dmv),
-        "write_backward",
-    )
     summed = sum_over_devices(
-        left, right, context, d_out, normed, pair, rest, gain, query_weight, key_weight,
-        value_weight,
+        later, memory, written, retain, vector, query_weight, out_weight, gain, memory_init, scan,
+        r, p, sq, k, v, left, mn, cr, cw, dr, dq, dk, dv, dmk, dmv, key_weight, value_weight,
     )
     grad_query, grad_out, grad_key, grad_value, grad_gain, grad_gate, grad_memory = local_kernel(
         finish_kernel,

time: 130 us -> 126 us (0.969)
  Pallas kernels: 127 us -> 124 us
    pallas_call x4 -> x3, Pallas kernels: 25.3 us -> 16.3 us  [local_kernel(): pl.pallas_call(kernel, out_shape=[jax.ShapeDtypeStruct(shape, dtype) for...]
    pallas_call x1, Pallas kernels: 53.7 us -> 59.8 us  [sum_over_devices(): pl.pallas_call(sum_kernel, out_shape=jax.ShapeDtypeStruct((8, TOTAL + 128...]
where the time goes in v5:
time: 126 us; the launch traced here: 125 us
  Pallas kernels  124 us (98%)
  between operations  1.3 us (1%)
    pallas_call x1, Pallas kernels, sum_over_devices(): pl.pallas_call(sum_kernel, out_shape=jax.ShapeDtypeStruct((8, TOTAL + 128...  59.8 us
    pallas_call x2, Pallas kernels, entering(): pl.pallas_call(functools.partial(scan_kernel, reverse), out_shape=jax.Sha...  47.9 us
    pallas_call x3, Pallas kernels, local_kernel(): pl.pallas_call(kernel, out_shape=[jax.ShapeDtypeStruct(shape, dtype) for...  16.3 us

profile of v5, /device:TPU:32, one launch (start us, length us, event | category | flops | bytes accessed | tf_op | source)
XLA Modules:
  0.0 125.3 jit_solution(10178579022112467148)
XLA Ops:
  1.3 6.0 %write_forward.1 = (bf16[128,1024]{1,0:T(8,128)(2,1)}, bf16[128,256]{1,0:T(8,128)(2,1)}, bf16[128,256]{1,0:T(8,128)(2,1)}, bf16[256,1024]{1,0:T(8,128)(2,1)}, bf...) custom-call(s32[1,1]{1,0:T(1,128)S(6)} %copy.19.length_ref, ...), custom_call_target="tpu_custom_call" | custom-call | tf_op jit(solution)/shard_map/write_forward/pallas_call | solution.py:717
  7.3 24.4 %prefix.1.scan_ref.refs_9_ = f32[128,1152]{1,0:T(8,128)} custom-call(f32[128,1024]{1,0:T(8,128)} %get-tuple-element.36.add_ref, f32[128,128]{1,0:T(8,128)} %get-tuple-element.37.keep_ref.refs_3_), custom_call_target="tpu_custom_call" | custom-call | tf_op jit(solution)/shard_map/prefix/pallas_call | solution.py:545
  31.7 8.7 %read_both.1 = (bf16[128,1024]{1,0:T(8,128)(2,1)}, f32[128,1024]{1,0:T(8,128)}, bf16[128,1024]{1,0:T(8,128)(2,1)}, bf16[128,1024]{1,0:T(8,128)(2,1)}, bf16[128,1...) custom-call(s32[1,1]{1,0:T(1,128)S(6)} %copy.19.length_ref, ...), custom_call_target="tpu_custom_call" | custom-call | tf_op jit(solution)/shard_map/read_both/pallas_call | solution.py:717
  40.4 23.5 %suffix.1.refs_0_ = f32[128,1152]{1,0:T(8,128)} custom-call(f32[128,1024]{1,0:T(8,128)} %get-tuple-element.42.add_ref.refs_10_, f32[128,128]{1,0:T(8,128)} %get-tuple-element.37.keep_ref.refs_3_), custom_call_target="tpu_custom_call" | custom-call | tf_op jit(solution)/shard_map/suffix/pallas_call | solution.py:545
  63.9 59.8 %sum_over_devices.1.full = f32[8,2944]{1,0:T(8,128)} custom-call(f32[128,1152]{1,0:T(8,128)} %suffix.1.refs_0_, f32[128,1024]{1,0:T(8,128)} %get-tuple-element.43.refs_1_, f32[128,1024]{1,0:T(8,128)} %get-tuple-element.44.refs_2_, f32[128,128]{1,0:T(8,128)} %get-tuple-element.37.keep_ref.refs_3_, f32[1,1024]{1,0:T(1,128)} %bitcast.16, ...), custom_call_target="tpu_custom_call" | custom-call | tf_op jit(solution)/shard_map/sum_over_devices/pallas_call | solution.py:404
  123.7 1.5 %finish.1 = (f32[4,1024]{1,0:T(4,128)}, f32[4,1024]{1,0:T(4,128)}, f32[4,256]{1,0:T(4,128)}, f32[4,256]{1,0:T(4,128)}, f32[1,4]{1,0:T(1,128)}, /*index=5*/f32[1,4]{1,0:T(1,128)}, f32[4,128]{1,0:T(4,128)}) custom-call(f32[8,2944]{1,0:T(8,128)} %sum_over_devices.1.full), custom_call_target="tpu_custom_call" | custom-call | tf_op jit(solution)/shard_map/finish/pallas_call | solution.py:717

commit v6 on v5

--- a/solution.py
+++ b/solution.py
@@ -122,8 +122,10 @@
             copy.wait_send()
 
 
-ORDERS = (("x", "y", "z"), ("y", "z", "x"), ("z", "x", "y"))
-PARTS = 6
+ORDERS = (
+    ("y", "z", "x"), ("y", "z", "x"), ("z", "x", "y"),
+    ("x", "y", "z"), ("x", "y", "z"), ("z", "x", "y"),
+)
 WIDTHS = (512, 512, 512, 512, 512, 256)
 TOTAL = 2816
 
@@ -191,7 +193,7 @@
     sources = tuple(products) + (rest,)
 
     def build_part(part):
-        order, work = ORDERS[part % 3], works[part]
+        order, work = ORDERS[part], works[part]
         half_width = WIDTHS[part] // 2
 
         def build(zl, carry):
@@ -229,7 +231,7 @@
             n = part * 3 + stage
             stages.append(
                 (Direct if stage else Ring)(
-                    ORDERS[part % 3][stage],
+                    ORDERS[part][stage],
                     works[part] if stage == 0 else rings_of[2 * (n - 1) + 1],
                     rings_of[2 * n],
                     rings_of[2 * n + 1],
@@ -240,7 +242,7 @@
         rings[part] = stages
         stages[0].first()
 
-    early, late = (0, 1, 2), (3, 4, 5)
+    early, late = (1, 4, 2), (0, 3, 5)
 
     def second(parts, stage):
         for part in parts:
@@ -306,12 +308,6 @@
 
     scale = jnp.asarray(score_scale, BF16)
     d_slot = jnp.concatenate(d_slots, axis=1) * scale
-    right[:SEG] = dq_ref[...] * scale
-    right[SEG:] = d_slot
-    product_and_push(0)
-    product_and_push(3)
-    second((1,), 0)
-    begin(0)
     pair[:SEG, :256] = added(dk_ref[...], jnp.concatenate(d_keys, axis=1))
     pair[:SEG, 256:] = added(dv_ref[...], jnp.concatenate(d_values, axis=1))
     pair[SEG:, :256] = dmk_ref[...]
@@ -319,9 +315,14 @@
     normed[:SEG] = left[:SEG]
     normed[SEG:] = mn_ref[...]
     product_and_push(2)
+    right[:SEG] = dq_ref[...] * scale
+    right[SEG:] = d_slot
+    product_and_push(0)
+    begin(2)
+    second((1, 4), 0)
+    product_and_push(3)
+    begin(0)
     begin(3)
-    begin(2)
-    second((4, 0), 0)
     d_sn = mul_nt(d_slot, wq_ref[...]).astype(BF16).astype(F32)
     start = start_ref[...].astype(F32)
     total = normalize_back(start, gain[...], d_sn) + scan_ref[:, 1024:1025] * r_ref[...]
@@ -334,17 +335,18 @@
     push_core(5, rest.at[:, 1 - core], landed[5])
     second((2,), 0)
     begin(5)
-    finish((1,), 0)
-    second((3,), 0)
-    finish((0, 2), 0)
+    finish((1, 4), 0)
+    second((0, 3), 0)
+    finish((2,), 0)
     second((5,), 0)
-    finish((4,), 0)
-    finish((1, 0, 2), 1)
-    finish((3, 5), 0)
-    finish((1, 0, 2), 2)
+    finish((1, 4), 1)
+    finish((0, 3), 0)
+    finish((2,), 1)
+    finish((5,), 0)
+    finish(early, 2)
     fold(early, 0)
-    finish((4, 5, 3), 1)
-    finish((4, 5, 3), 2)
+    finish(late, 1)
+    finish(late, 2)
     fold(late, 1)
     for copy in core_copies:
         copy.wait_send()
@@ -371,8 +373,7 @@
         pieces += [short, pltpu.roll(short, 4, 0)]
     full = jnp.concatenate(pieces, axis=1)
     of_gain = (
-        jnp.sum(weights[0][:, :512] * full[:, :512], axis=1, keepdims=True)
-        + jnp.sum(weights[0][:, 512:] * full[:, 1536:2048], axis=1, keepdims=True)
+        jnp.sum(weights[0] * full[:, 1536:2560], axis=1, keepdims=True)
         + jnp.sum(weights[1] * full[:, 1024:1280], axis=1, keepdims=True)
         + jnp.sum(weights[2] * full[:, 1280:1536], axis=1, keepdims=True)
     ) / gains
@@ -415,10 +416,8 @@
 
 
 def finish_kernel(full, gq, go, gk, gv, gain, gate, memory):
-    gq[:, :512] = full[:4, :512]
-    gq[:, 512:] = full[:4, 1536:2048]
-    go[:, :512] = full[:4, 512:1024]
-    go[:, 512:] = full[:4, 2048:2560]
+    gq[...] = full[:4, 1536:2560]
+    go[...] = full[:4, :1024]
     gk[...] = full[:4, 1024:1280]
     gv[...] = full[:4, 1280:1536]
     memory[...] = full[:4, 2560:2688]

time: 126 us -> 123 us (0.976)
  Pallas kernels: 124 us -> 121 us
    pallas_call x1, Pallas kernels: 59.8 us -> 56.9 us  [sum_over_devices(): pl.pallas_call(sum_kernel, out_shape=jax.ShapeDtypeStruct((8, TOTAL + 128...]
where the time goes in v6:
time: 123 us; the launch traced here: 122 us
  Pallas kernels  121 us (98%)
  between operations  1.3 us (1%)
    pallas_call x1, Pallas kernels, sum_over_devices(): pl.pallas_call(sum_kernel, out_shape=jax.ShapeDtypeStruct((8, TOTAL + 128...  56.9 us
    pallas_call x2, Pallas kernels, entering(): pl.pallas_call(functools.partial(scan_kernel, reverse), out_shape=jax.Sha...  47.9 us
    pallas_call x3, Pallas kernels, local_kernel(): pl.pallas_call(kernel, out_shape=[jax.ShapeDtypeStruct(shape, dtype) for...  16.3 us

profile of v6, /device:TPU:32, one launch (start us, length us, event | category | flops | bytes accessed | tf_op | source)
XLA Modules:
  0.0 122.4 jit_solution(4162375259868677770)
XLA Ops:
  1.3 6.0 %write_forward.1 = (bf16[128,1024]{1,0:T(8,128)(2,1)}, bf16[128,256]{1,0:T(8,128)(2,1)}, bf16[128,256]{1,0:T(8,128)(2,1)}, bf16[256,1024]{1,0:T(8,128)(2,1)}, bf...) custom-call(s32[1,1]{1,0:T(1,128)S(6)} %copy.19.length_ref, ...), custom_call_target="tpu_custom_call" | custom-call | tf_op jit(solution)/shard_map/write_forward/pallas_call | solution.py:716
  7.3 24.4 %prefix.1.scan_ref.refs_9_ = f32[128,1152]{1,0:T(8,128)} custom-call(f32[128,1024]{1,0:T(8,128)} %get-tuple-element.36.add_ref, f32[128,128]{1,0:T(8,128)} %get-tuple-element.37.keep_ref.refs_3_), custom_call_target="tpu_custom_call" | custom-call | tf_op jit(solution)/shard_map/prefix/pallas_call | solution.py:544
  31.7 8.7 %read_both.1 = (bf16[128,1024]{1,0:T(8,128)(2,1)}, f32[128,1024]{1,0:T(8,128)}, bf16[128,1024]{1,0:T(8,128)(2,1)}, bf16[128,1024]{1,0:T(8,128)(2,1)}, bf16[128,1...) custom-call(s32[1,1]{1,0:T(1,128)S(6)} %copy.19.length_ref, ...), custom_call_target="tpu_custom_call" | custom-call | tf_op jit(solution)/shard_map/read_both/pallas_call | solution.py:716
  40.4 23.5 %suffix.1.refs_0_ = f32[128,1152]{1,0:T(8,128)} custom-call(f32[128,1024]{1,0:T(8,128)} %get-tuple-element.42.add_ref.refs_10_, f32[128,128]{1,0:T(8,128)} %get-tuple-element.37.keep_ref.refs_3_), custom_call_target="tpu_custom_call" | custom-call | tf_op jit(solution)/shard_map/suffix/pallas_call | solution.py:544
  63.9 56.9 %sum_over_devices.1.full = f32[8,2944]{1,0:T(8,128)} custom-call(f32[128,1152]{1,0:T(8,128)} %suffix.1.refs_0_, f32[128,1024]{1,0:T(8,128)} %get-tuple-element.43.refs_1_, f32[128,1024]{1,0:T(8,128)} %get-tuple-element.44.refs_2_, f32[128,128]{1,0:T(8,128)} %get-tuple-element.37.keep_ref.refs_3_, f32[1,1024]{1,0:T(1,128)} %bitcast.16, ...), custom_call_target="tpu_custom_call" | custom-call | tf_op jit(solution)/shard_map/sum_over_devices/pallas_call | solution.py:405
  120.8 1.5 %finish.1 = (f32[4,1024]{1,0:T(4,128)}, f32[4,1024]{1,0:T(4,128)}, f32[4,256]{1,0:T(4,128)}, f32[4,256]{1,0:T(4,128)}, f32[1,4]{1,0:T(1,128)}, /*index=5*/f32[1,4]{1,0:T(1,128)}, f32[4,128]{1,0:T(4,128)}) custom-call(f32[8,2944]{1,0:T(8,128)} %sum_over_devices.1.full), custom_call_target="tpu_custom_call" | custom-call | tf_op jit(solution)/shard_map/finish/pallas_call | solution.py:716

commit v7 on v6

--- a/solution.py
+++ b/solution.py
@@ -124,7 +124,7 @@
 
 ORDERS = (
     ("y", "z", "x"), ("y", "z", "x"), ("z", "x", "y"),
-    ("x", "y", "z"), ("x", "y", "z"), ("z", "x", "y"),
+    ("x", "y", "z"), ("x", "z", "y"), ("z", "x", "y"),
 )
 WIDTHS = (512, 512, 512, 512, 512, 256)
 TOTAL = 2816
@@ -132,12 +132,12 @@
 
 def sum_kernel(*refs):
     (
-        later_ref, memory_ref, written_ref, retain_ref, vector_ref, wq_ref, wo_ref, gain,
+        later_ref, memory_ref, written_ref, retain_ref, vector_ref, gain,
         start_ref, scan_ref, r_ref, p_ref, sq_ref, k_ref, v_ref, left, mn_ref,
-        cr_ref, cw_ref, dr_ref, dq_ref, dk_ref, dv_ref, dmk_ref, dmv_ref, wk, wv,
+        cr_ref, cw_ref, dr_ref, dq_ref, dk_ref, dv_ref, dmk_ref, dmv_ref, wk, wv, wo, wq,
     ) = refs[:27]
     out_ref, refs = refs[27], refs[28:]
-    right, context, d_out, normed, pair, rest, *refs = refs
+    wo_ref, wq_ref, right, context, d_out, normed, pair, rest, *refs = refs
     products, refs = refs[:5], refs[5:]
     landed, refs = refs[:6], refs[6:]
     works, refs = refs[:6], refs[6:]
@@ -154,7 +154,11 @@
         pltpu.make_async_copy(w.at[base], rows, row_sems.at[k])
         for k, (w, rows) in enumerate(zip((wk, wv), rows_of))
     ]
-    for copy in row_copies:
+    whole_copies = [
+        pltpu.make_async_copy(wo, wo_ref, row_sems.at[2]),
+        pltpu.make_async_copy(wq, wq_ref, row_sems.at[3]),
+    ]
+    for copy in whole_copies + row_copies:
         copy.start()
     peers = [other, far, shift("x", 2), shift("y", 2), shift("z", 2), shift("z", -2)]
     peers += [shift(axis, step) for axis in ("x", "y", "z") for step in (1, -1)]
@@ -290,6 +294,7 @@
     product_and_push(4)
     begin(1)
     begin(4)
+    whole_copies[0].wait()
     d_context = mul_nt(d_written, wo_ref[...]).astype(BF16)
     slots, keys, values = sq_ref[...], k_ref[...], v_ref[...]
     d_slots, d_keys, d_values = [], [], []
@@ -323,6 +328,7 @@
     product_and_push(3)
     begin(0)
     begin(3)
+    whole_copies[1].wait()
     d_sn = mul_nt(d_slot, wq_ref[...]).astype(BF16).astype(F32)
     start = start_ref[...].astype(F32)
     total = normalize_back(start, gain[...], d_sn) + scan_ref[:, 1024:1025] * r_ref[...]
@@ -383,7 +389,7 @@
 
 def sum_over_devices(*operands):
     tall = pltpu.VMEM((2 * SEG, 1024), BF16)
-    scratch = [tall] * 4 + [pltpu.VMEM((2 * SEG, 512), BF16), pltpu.VMEM((16, 2, 32, 256), F32)]
+    scratch = [pltpu.VMEM((1024, 1024), BF16)] * 2 + [tall] * 4 + [pltpu.VMEM((2 * SEG, 512), BF16), pltpu.VMEM((16, 2, 32, 256), F32)]
     scratch += [pltpu.VMEM((16, 2, 32, n), F32) for n in WIDTHS[:5]]
     scratch += [pltpu.VMEM((16, 32, n), F32) for n in WIDTHS]
     scratch += [pltpu.VMEM((2, 4, 4, 4, 8, n // 2), F32) for n in WIDTHS]
@@ -400,12 +406,12 @@
         pltpu.SemaphoreType.DMA((18, 6)),
         pltpu.SemaphoreType.DMA((18, 6)),
         pltpu.SemaphoreType.DMA((2, 2)),
-        pltpu.SemaphoreType.DMA((3,)),
+        pltpu.SemaphoreType.DMA((4,)),
     ]
     return pl.pallas_call(
         sum_kernel,
         out_shape=jax.ShapeDtypeStruct((8, TOTAL + 128), F32),
-        in_specs=[VMEM_SPEC] * 25 + [pl.BlockSpec(memory_space=pl.ANY)] * 2,
+        in_specs=[VMEM_SPEC] * 23 + [pl.BlockSpec(memory_space=pl.ANY)] * 4,
         out_specs=VMEM_SPEC,
         scratch_shapes=scratch,
         compiler_params=pltpu.CompilerParams(
@@ -758,8 +764,8 @@
     )
     later = entering(retain, r, True)
     summed = sum_over_devices(
-        later, memory, written, retain, vector, query_weight, out_weight, gain, memory_init, scan,
-        r, p, sq, k, v, left, mn, cr, cw, dr, dq, dk, dv, dmk, dmv, key_weight, value_weight,
+        later, memory, written, retain, vector, gain, memory_init, scan, r, p, sq, k, v, left, mn,
+        cr, cw, dr, dq, dk, dv, dmk, dmv, key_weight, value_weight, out_weight, query_weight,
     )
     grad_query, grad_out, grad_key, grad_value, grad_gain, grad_gate, grad_memory = local_kernel(
         finish_kernel,

time: 123 us -> 125 us (1.016)
  Pallas kernels: 121 us -> 123 us
    pallas_call x1, Pallas kernels: 56.9 us -> 58.8 us  [sum_over_devices(): pl.pallas_call(sum_kernel, out_shape=jax.ShapeDtypeStruct((8, TOTAL + 128...]
where the time goes in v7:
time: 125 us; the launch traced here: 124 us
  Pallas kernels  123 us (98%)
  between operations  1.3 us (1%)
    pallas_call x1, Pallas kernels, sum_over_devices(): pl.pallas_call(sum_kernel, out_shape=jax.ShapeDtypeStruct((8, TOTAL + 128...  58.8 us
    pallas_call x2, Pallas kernels, entering(): pl.pallas_call(functools.partial(scan_kernel, reverse), out_shape=jax.Sha...  47.9 us
    pallas_call x3, Pallas kernels, local_kernel(): pl.pallas_call(kernel, out_shape=[jax.ShapeDtypeStruct(shape, dtype) for...  16.3 us

profile of v7, /device:TPU:32, one launch (start us, length us, event | category | flops | bytes accessed | tf_op | source)
XLA Modules:
  0.0 124.3 jit_solution(11228044340429653741)
XLA Ops:
  1.3 6.0 %write_forward.1 = (bf16[128,1024]{1,0:T(8,128)(2,1)}, bf16[128,256]{1,0:T(8,128)(2,1)}, bf16[128,256]{1,0:T(8,128)(2,1)}, bf16[256,1024]{1,0:T(8,128)(2,1)}, bf...) custom-call(s32[1,1]{1,0:T(1,128)S(6)} %copy.19.length_ref, ...), custom_call_target="tpu_custom_call" | custom-call | tf_op jit(solution)/shard_map/write_forward/pallas_call | solution.py:722
  7.3 24.4 %prefix.1.scan_ref.refs_7_ = f32[128,1152]{1,0:T(8,128)} custom-call(f32[128,1024]{1,0:T(8,128)} %get-tuple-element.36.add_ref, f32[128,128]{1,0:T(8,128)} %get-tuple-element.37.keep_ref.refs_3_), custom_call_target="tpu_custom_call" | custom-call | tf_op jit(solution)/shard_map/prefix/pallas_call | solution.py:550
  31.7 8.7 %read_both.1 = (bf16[128,1024]{1,0:T(8,128)(2,1)}, f32[128,1024]{1,0:T(8,128)}, bf16[128,1024]{1,0:T(8,128)(2,1)}, bf16[128,1024]{1,0:T(8,128)(2,1)}, bf16[128,1...) custom-call(s32[1,1]{1,0:T(1,128)S(6)} %copy.19.length_ref, ...), custom_call_target="tpu_custom_call" | custom-call | tf_op jit(solution)/shard_map/read_both/pallas_call | solution.py:722
  40.4 23.5 %suffix.1.refs_0_ = f32[128,1152]{1,0:T(8,128)} custom-call(f32[128,1024]{1,0:T(8,128)} %get-tuple-element.42.add_ref.refs_8_, f32[128,128]{1,0:T(8,128)} %get-tuple-element.37.keep_ref.refs_3_), custom_call_target="tpu_custom_call" | custom-call | tf_op jit(solution)/shard_map/suffix/pallas_call | solution.py:550
  63.9 58.8 %sum_over_devices.1.full = f32[8,2944]{1,0:T(8,128)} custom-call(f32[128,1152]{1,0:T(8,128)} %suffix.1.refs_0_, f32[128,1024]{1,0:T(8,128)} %get-tuple-element.43.refs_1_, f32[128,1024]{1,0:T(8,128)} %get-tuple-element.44.refs_2_, f32[128,128]{1,0:T(8,128)} %get-tuple-element.37.keep_ref.refs_3_, f32[1,1024]{1,0:T(1,128)} %bitcast.16, f32[1,1024]{1,0:T(1,128)} %bitcast.14, ...), custom_call_target="tpu_custom_call" | custom-call | tf_op jit(solution)/shard_map/sum_over_devices/pallas_call | solution.py:411
  122.8 1.5 %finish.1 = (f32[4,1024]{1,0:T(4,128)}, f32[4,1024]{1,0:T(4,128)}, f32[4,256]{1,0:T(4,128)}, f32[4,256]{1,0:T(4,128)}, f32[1,4]{1,0:T(1,128)}, /*index=5*/f32[1,4]{1,0:T(1,128)}, f32[4,128]{1,0:T(4,128)}) custom-call(f32[8,2944]{1,0:T(8,128)} %sum_over_devices.1.full), custom_call_target="tpu_custom_call" | custom-call | tf_op jit(solution)/shard_map/finish/pallas_call | solution.py:722
